TPU v7x, 32 devices: a whole 2x2x4 slice. The times are simulated.
32 devices in a mesh: vec: 16 (over z, y, x), row: 2 (over core).
Axes of the slice: x: 2, y: 2, z: 4, core: 2. Of those that a mesh axis runs over, the one named last changes fastest.
Arguments:
- vectors: bfloat16 [2, 4096, 1024], P('row', 'vec'), may hold values from -6 to 6
- rotation: bfloat16 [1024, 1024], P(None, 'vec'), may hold values from -0.1875 to 0.1875
- blocks: bfloat16 [64, 8, 128, 128], P('row'), may hold values from -0.125 to 0.125
- column_blocks: int32 [64, 8], P('row'), may hold values from -2 to 65, as said below
Outputs:
- filtered: bfloat16 [2, 4096, 1024], P('row', 'vec')
Inputs may be any that keep to these rules, and one draw needn't show every extreme that they name: `column_blocks`: block row r of partition p = r // 32 lists 8 distinct column blocks between p * 32 - 2 and p * 32 + 33; the first block row of every partition lists the lowest of these and the last one the highest; column blocks outside 0 to 63 stand for zeros.
All inputs are finite; a program needn't handle non-finite values.
Results may differ from a plain program's by a relative error of at most 0.006.
Values may be sent and summed in bfloat16 or wider, within the bound.
No kernel may reach another device: no remote copies, remote signals or barrier semaphores. Data moves between devices by JAX's collectives and lax.ppermute only.
A program may use at most 64 MiB of HBM per device.

v0:
```python
import jax
import jax.numpy as jnp
from jax import lax
from jax.sharding import PartitionSpec as P

BS = 128
HB = 2
STEPS = 4


centre = 0.3
half_width = 1.2


def with_halo(block, sides, width):
    for axis, dim in sides:
        count = lax.axis_size(axis)
        forward = [(i, i + 1) for i in range(count - 1)]
        backward = [(target, source) for source, target in forward]
        low = lax.ppermute(
            lax.slice_in_dim(block, block.shape[dim] - width, None, axis=dim), axis, forward
        )
        high = lax.ppermute(lax.slice_in_dim(block, 0, width, axis=dim), axis, backward)
        block = jnp.concatenate([low, block, high], axis=dim)
    return block


def apply_matrix(operand, blocks, offsets):
    extended = with_halo(operand, (("row", 1),), HB * BS)
    stacked = extended.reshape(extended.shape[0], -1, BS)
    picked = stacked[:, offsets]
    product = jnp.einsum("rjab,krjb->kra", blocks, picked, preferred_element_type=jnp.float32)
    return product.reshape(extended.shape[0], -1)


def filter_panel(vec_panel, blocks, offsets):
    previous = vec_panel.astype(jnp.float32)
    current = (apply_matrix(vec_panel, blocks, offsets) - centre * previous) / half_width
    for turn_index in range(STEPS - 1):
        operand = current.astype(jnp.bfloat16)
        following = (
            2.0 * (apply_matrix(operand, blocks, offsets) - centre * current) / half_width
            - previous
        )
        previous = current
        current = following
    return current.astype(jnp.bfloat16)


def local(vectors, rotation, blocks, column_blocks):
    local_rows = vectors[0]
    offsets = column_blocks - (lax.axis_index("row") * column_blocks.shape[0] - HB)
    contract = (((0,), (1,)), ((), ()))
    rotated = lax.dot_general(
        lax.all_gather(rotation, "vec", axis=1, tiled=True),
        local_rows,
        contract,
        preferred_element_type=jnp.float32,
    ).astype(jnp.bfloat16)
    vec_panel = lax.all_to_all(rotated, "vec", split_axis=0, concat_axis=1, tiled=True)
    filtered = filter_panel(vec_panel, blocks, offsets)
    returned = lax.all_to_all(filtered, "vec", split_axis=1, concat_axis=0, tiled=True)
    return jnp.transpose(returned)[None]


def solution(mesh):
    placed = (P("row", "vec", None), P(None, "vec"), P("row", None, None, None), P("row", None))
    return jax.shard_map(
        local, mesh=mesh, in_specs=placed, out_specs=P("row", "vec", None), check_vma=False
    )
```

profile of v0, /device:TPU:0, one launch (start us, length us, event | category | flops | bytes accessed | tf_op | source)
XLA Modules:
  0.0 203.2 jit_solution(18180730329563429137)
XLA Ops:
  7.3 66.0 %all-gather.2.cloned.1.call-done = bf16[1024,1024]{0,1:T(8,128)(2,1)} async-done(((bf16[1024,64]{0,1:T(8,128)(2,1)}), bf16[1024,1024]{0,1:T(8,128)(2,1)}) %all-gather.2.cloned.1.call-update) | async-done | bytes 2097168 | tf_op jit(solution)/shard_map/all_gather | solution.py:55
  73.2 3.1 %convolution_convert_fusion = bf16[1024,256]{1,0:T(8,128)(2,1)} fusion(bf16[1024,1024]{0,1:T(8,128)(2,1)} %all-gather.2.cloned.1.call-done, bf16[1,256,1024]{2,1,0:T(8,128)(2,1)S(1)} %copy-done), kind=kOutput, calls=%fused_computation.9 | convolution fusion | flops 537133056 | bytes 3145728 | tf_op jit(solution)/shard_map/dot_general | solution.py:54
  76.4 4.4 %all-to-all-start = ((bf16[16,64,256]{2,1,0:T(8,128)(2,1)}), bf16[16,64,256]{2,1,0:T(8,128)(2,1)S(1)}, u32[]{:S(2)}, u32[]{:S(2)}) async-start(bf16[16,64,256]{2,1,0:T(8,128)(2,1)} %bitcast.1), calls=%async_computation | async-start | bytes 1048576 | tf_op jit(solution)/shard_map/all_to_all | solution.py:60
  81.0 14.0 %all-to-all-done = bf16[16,64,256]{2,1,0:T(8,128)(2,1)S(1)} async-done(((bf16[16,64,256]{2,1,0:T(8,128)(2,1)}), bf16[16,64,256]{2,1,0:T(8,128)(2,1)S(1)}, u32[]{:S(2)}, u32[]{:S(2)}) %all-to-all-start) | async-done | bytes 524320 | tf_op jit(solution)/shard_map/all_to_all | solution.py:60
  96.3 1.3 collective-permute-start.1
  97.7 1.8 collective-permute-done.1
  99.6 3.0 %gather_fusion = bf16[256,64,128]{2,1,0:T(8,128)(2,1)} fusion(bf16[64,36,128]{2,0,1:T(8,128)(2,1)S(1)} %copy_bitcast_fusion.3, s32[1024]{0:T(1024)S(1)} %pad_clamp_fusion), kind=kCustom, calls=%fused_computation | custom fusion | bytes 8389632 | tf_op jit(solution)/shard_map/gather | solution.py:31
  102.7 7.6 %fusion.12 = f32[32,64,128,1]{2,1,3,0:T(8,128)S(1)} fusion(bf16[64,32,8,128]{3,0,2,1:T(8,128)(2,1)} %bitcast.117, bf16[32,8,128,128]{3,2,1,0:T(8,128)(2,1)} %param.6), kind=kOutput, calls=%fused_computation.36 | convolution fusion | flops 536870912 | bytes 13631488 | tf_op jit(solution)/shard_map/rjab,krjb->kra/dot_general | solution.py:32
  110.5 2.1 %collective-permute-start.2 = (bf16[64,256]{1,0:T(8,128)(2,1)S(1)}, bf16[64,256]{1,0:T(8,128)(2,1)S(1)}, u32[]{:S(2)}, u32[]{:S(2)}) collective-permute-start(bf16[64,256]{1,0:T(8,128)(2,1)S(1)} %get-tuple-element.9), channel_id=1, source_target_pairs={{0,1},{2,3},{4,5},{6,7},{8,9},{10,11},{12,13},{14,15},{16,17},{18,... | collective-permute-start | bytes 98312 | tf_op jit(solution)/shard_map/ppermute | solution.py:20
  112.5 1.3 collective-permute-start.3
  113.8 1.8 collective-permute-done.3
  115.8 3.0 %gather_fusion.1 = bf16[256,64,128]{2,1,0:T(8,128)(2,1)} fusion(bf16[64,36,128]{2,0,1:T(8,128)(2,1)S(1)} %copy_bitcast_fusion.2, s32[1024]{0:T(1024)S(1)} %pad_clamp_fusion), kind=kCustom, calls=%fused_computation.1 | custom fusion | bytes 8389632 | tf_op jit(solution)/shard_map/gather | solution.py:31
  118.8 7.6 %fusion.13 = f32[32,64,128,1]{2,1,3,0:T(8,128)S(1)} fusion(bf16[64,32,8,128]{3,0,2,1:T(8,128)(2,1)} %bitcast.118, bf16[32,8,128,128]{3,2,1,0:T(8,128)(2,1)} %param.6), kind=kOutput, calls=%fused_computation.37 | convolution fusion | flops 536870912 | bytes 13631488 | tf_op jit(solution)/shard_map/rjab,krjb->kra/dot_general | solution.py:32
  126.8 2.1 %collective-permute-start.4 = (bf16[64,256]{1,0:T(8,128)(2,1)S(1)}, bf16[64,256]{1,0:T(8,128)(2,1)S(1)}, u32[]{:S(2)}, u32[]{:S(2)}) collective-permute-start(bf16[64,256]{1,0:T(8,128)(2,1)S(1)} %get-tuple-element.7), channel_id=1, source_target_pairs={{0,1},{2,3},{4,5},{6,7},{8,9},{10,11},{12,13},{14,15},{16,17},{18,... | collective-permute-start | bytes 98312 | tf_op jit(solution)/shard_map/ppermute | solution.py:20
  128.9 1.3 collective-permute-start.5
  130.2 1.8 collective-permute-done.5
  132.1 3.0 %gather_fusion.2 = bf16[256,64,128]{2,1,0:T(8,128)(2,1)} fusion(bf16[64,36,128]{2,0,1:T(8,128)(2,1)S(1)} %copy_bitcast_fusion.1, s32[1024]{0:T(1024)S(1)} %pad_clamp_fusion), kind=kCustom, calls=%fused_computation.2 | custom fusion | bytes 8389632 | tf_op jit(solution)/shard_map/gather | solution.py:31
  135.2 7.6 %fusion.14 = f32[32,64,128,1]{2,1,3,0:T(8,128)S(1)} fusion(bf16[64,32,8,128]{3,0,2,1:T(8,128)(2,1)} %bitcast.119, bf16[32,8,128,128]{3,2,1,0:T(8,128)(2,1)} %param.6), kind=kOutput, calls=%fused_computation.38 | convolution fusion | flops 536870912 | bytes 13631488 | tf_op jit(solution)/shard_map/rjab,krjb->kra/dot_general | solution.py:32
  143.8 2.1 %collective-permute-start.6 = (bf16[64,256]{1,0:T(8,128)(2,1)S(1)}, bf16[64,256]{1,0:T(8,128)(2,1)S(1)}, u32[]{:S(2)}, u32[]{:S(2)}) collective-permute-start(bf16[64,256]{1,0:T(8,128)(2,1)S(1)} %get-tuple-element.5), channel_id=1, source_target_pairs={{0,1},{2,3},{4,5},{6,7},{8,9},{10,11},{12,13},{14,15},{16,17},{18,... | collective-permute-start | bytes 98312 | tf_op jit(solution)/shard_map/ppermute | solution.py:20
  145.9 1.5 collective-permute-start.7
  147.4 1.6 copy.24
  149.0 2.6 %reshape.50 = f32[64,16,256]{2,1,0:T(8,128)} reshape(f32[64,32,128]{2,1,0:T(8,128)} %copy.24) | data formatting | bytes 2097152 | tf_op jit(solution)/shard_map/reshape | solution.py:33
  151.6 1.6 copy.26
  153.2 1.5 reshape.49
  154.7 1.6 copy.28
  156.3 2.5 %reshape.48 = f32[64,16,256]{2,1,0:T(8,128)} reshape(f32[64,32,128]{2,1,0:T(8,128)} %copy.28) | data formatting | bytes 2097152 | tf_op jit(solution)/shard_map/reshape | solution.py:33
  159.0 3.0 %gather_fusion.3 = bf16[256,64,128]{2,1,0:T(8,128)(2,1)} fusion(bf16[64,36,128]{2,0,1:T(8,128)(2,1)S(1)} %copy_bitcast_fusion, s32[1024]{0:T(1024)S(1)} %pad_clamp_fusion), kind=kCustom, calls=%fused_computation.3 | custom fusion | bytes 8389632 | tf_op jit(solution)/shard_map/gather | solution.py:31
  162.1 7.6 %convolution_bitcast_fusion = f32[64,32,128]{2,0,1:T(8,128)S(1)} fusion(bf16[64,32,8,128]{3,0,2,1:T(8,128)(2,1)} %bitcast.116, bf16[32,8,128,128]{3,2,1,0:T(8,128)(2,1)} %param.6), kind=kOutput, calls=%fused_computation.4 | convolution fusion | flops 536870912 | bytes 13631488 | tf_op jit(solution)/shard_map/rjab,krjb->kra/dot_general | solution.py:32
  169.7 1.6 copy.30
  171.3 2.5 %reshape.47 = f32[64,16,256]{2,1,0:T(8,128)} reshape(f32[64,32,128]{2,1,0:T(8,128)} %copy.30) | data formatting | bytes 2097152 | tf_op jit(solution)/shard_map/reshape | solution.py:33
  173.8 2.4 %subtract_convert_fusion = bf16[64,16,256]{2,1,0:T(8,128)(2,1)S(1)} fusion(f32[64,16,256]{2,1,0:T(8,128)} %reshape.47, f32[64,16,256]{2,1,0:T(8,128)} %reshape.48, f32[64,16,256]{2,1,0:T(8,128)S(1)} %reshape.49, f32[64,16,256]{2,1,0:T(8,128)S(1)} %copy-done.8, bf16[16,64,256]{2,1,0:T(8,128)(2,1)S(1)} %copy-done.7), kind=kLoop, calls=%fused_computation.18 | loop fusion | flops 4456448 | bytes 5242880 | tf_op jit(solution)/shard_map/convert_element_type | solution.py:47
  176.3 19.0 %all_to_all.35 = bf16[64,16,256]{2,0,1:T(8,128)(2,1)S(1)} all-to-all(bf16[64,16,256]{2,0,1:T(8,128)(2,1)S(1)} %copy.34), channel_id=1, replica_groups=mesh['vec'=16,'row'=2] {'vec'}, dimensions={1} | all-to-all | bytes 1048576 | tf_op jit(solution)/shard_map/all_to_all | solution.py:62
  (50 shorter events, 5.5 us)
Async XLA Ops:
  6.5 66.7 %copy-start = (bf16[1,256,1024]{2,1,0:T(8,128)(2,1)S(1)}, bf16[1,256,1024]{2,1,0:T(8,128)(2,1)}, u32[]{:S(2)}) copy-start(bf16[1,256,1024]{2,1,0:T(8,128)(2,1)} %param.4) | copy-start | bytes 1572868
  6.5 74.3 %copy-start.11 = (s32[32,8]{0,1:T(8,128)S(1)}, s32[32,8]{0,1:T(8,128)}, u32[]{:S(2)}) copy-start(s32[32,8]{0,1:T(8,128)} %param.7) | copy-start | bytes 3076
  6.5 66.7 %all-gather.2.cloned.1.call-start = ((), (), s32[]{:S(2)}) async-start(), calls=%async_computation.2 | async-start | bytes 2228224 | tf_op jit(solution)/shard_map/all_gather | solution.py:55
  76.4 18.6 %all-to-all-start = ((bf16[16,64,256]{2,1,0:T(8,128)(2,1)}), bf16[16,64,256]{2,1,0:T(8,128)(2,1)S(1)}, u32[]{:S(2)}, u32[]{:S(2)}) async-start(bf16[16,64,256]{2,1,0:T(8,128)(2,1)} %bitcast.1), calls=%async_computation | async-start | bytes 1048576 | tf_op jit(solution)/shard_map/all_to_all | solution.py:60
  95.0 2.7 %copy-start.6 = (bf16[16,64,256]{2,1,0:T(8,128)(2,1)}, bf16[16,64,256]{2,1,0:T(8,128)(2,1)S(1)}, u32[]{:S(2)}) copy-start(bf16[16,64,256]{2,1,0:T(8,128)(2,1)S(1)} %all-to-all-done) | copy-start | bytes 1572868
  95.0 15.2 %copy-start.1 = (bf16[8,8,16,256]{3,1,2,0:T(8,128)(2,1)}, bf16[8,8,16,256]{3,1,2,0:T(8,128)(2,1)S(1)}, u32[]{:S(2)}) copy-start(bf16[8,8,16,256]{3,1,2,0:T(8,128)(2,1)S(1)} %copy.47) | copy-start | bytes 1572868
  95.0 2.6 %collective-permute-start = (bf16[64,256]{1,0:T(8,128)(2,1)S(1)}, bf16[64,256]{1,0:T(8,128)(2,1)S(1)}, u32[]{:S(2)}, u32[]{:S(2)}) collective-permute-start(bf16[64,256]{1,0:T(8,128)(2,1)S(1)} %get-tuple-element.11), channel_id=1, source_target_pairs={{0,1},{2,3},{4,5},{6,7},{8,9},{10,11},{12,13},{14,15},{16,17},{18,... | collective-permute-start | bytes 98312 | tf_op jit(solution)/shard_map/ppermute | solution.py:20
  96.3 3.1 %collective-permute-start.1 = (bf16[64,256]{1,0:T(8,128)(2,1)S(1)}, bf16[64,256]{1,0:T(8,128)(2,1)S(1)}, u32[]{:S(2)}, u32[]{:S(2)}) collective-permute-start(bf16[64,256]{1,0:T(8,128)(2,1)S(1)} %get-tuple-element.12), channel_id=1, source_target_pairs={{1,0},{3,2},{5,4},{7,6},{9,8},{11,10},{13,12},{15,14},{17,16},{19,... | collective-permute-start | bytes 98312 | tf_op jit(solution)/shard_map/ppermute | solution.py:23
  110.5 3.4 %collective-permute-start.2 = (bf16[64,256]{1,0:T(8,128)(2,1)S(1)}, bf16[64,256]{1,0:T(8,128)(2,1)S(1)}, u32[]{:S(2)}, u32[]{:S(2)}) collective-permute-start(bf16[64,256]{1,0:T(8,128)(2,1)S(1)} %get-tuple-element.9), channel_id=1, source_target_pairs={{0,1},{2,3},{4,5},{6,7},{8,9},{10,11},{12,13},{14,15},{16,17},{18,... | collective-permute-start | bytes 98312 | tf_op jit(solution)/shard_map/ppermute | solution.py:20
  112.5 3.1 %collective-permute-start.3 = (bf16[64,256]{1,0:T(8,128)(2,1)S(1)}, bf16[64,256]{1,0:T(8,128)(2,1)S(1)}, u32[]{:S(2)}, u32[]{:S(2)}) collective-permute-start(bf16[64,256]{1,0:T(8,128)(2,1)S(1)} %get-tuple-element.10), channel_id=1, source_target_pairs={{1,0},{3,2},{5,4},{7,6},{9,8},{11,10},{13,12},{15,14},{17,16},{19,... | collective-permute-start | bytes 98312 | tf_op jit(solution)/shard_map/ppermute | solution.py:23
  118.8 7.7 %copy-start.2 = (bf16[8,8,16,256]{3,1,2,0:T(8,128)(2,1)S(1)}, bf16[8,8,16,256]{3,1,2,0:T(8,128)(2,1)}, u32[]{:S(2)}) copy-start(bf16[8,8,16,256]{3,1,2,0:T(8,128)(2,1)} %copy-done.1) | copy-start | bytes 1572868
  126.8 3.4 %collective-permute-start.4 = (bf16[64,256]{1,0:T(8,128)(2,1)S(1)}, bf16[64,256]{1,0:T(8,128)(2,1)S(1)}, u32[]{:S(2)}, u32[]{:S(2)}) collective-permute-start(bf16[64,256]{1,0:T(8,128)(2,1)S(1)} %get-tuple-element.7), channel_id=1, source_target_pairs={{0,1},{2,3},{4,5},{6,7},{8,9},{10,11},{12,13},{14,15},{16,17},{18,... | collective-permute-start | bytes 98312 | tf_op jit(solution)/shard_map/ppermute | solution.py:20
  128.9 3.1 %collective-permute-start.5 = (bf16[64,256]{1,0:T(8,128)(2,1)S(1)}, bf16[64,256]{1,0:T(8,128)(2,1)S(1)}, u32[]{:S(2)}, u32[]{:S(2)}) collective-permute-start(bf16[64,256]{1,0:T(8,128)(2,1)S(1)} %get-tuple-element.8), channel_id=1, source_target_pairs={{1,0},{3,2},{5,4},{7,6},{9,8},{11,10},{13,12},{15,14},{17,16},{19,... | collective-permute-start | bytes 98312 | tf_op jit(solution)/shard_map/ppermute | solution.py:23
  135.2 7.7 %copy-start.3 = (bf16[8,8,16,256]{3,1,2,0:T(8,128)(2,1)S(1)}, bf16[8,8,16,256]{3,1,2,0:T(8,128)(2,1)}, u32[]{:S(2)}) copy-start(bf16[8,8,16,256]{3,1,2,0:T(8,128)(2,1)} %copy-done.1) | copy-start | bytes 1572868
  142.8 1.0 copy-start.4
  143.8 3.6 %copy-start.9 = (bf16[64,4096]{1,0:T(8,128)(2,1)}, bf16[64,4096]{1,0:T(8,128)(2,1)S(1)}, u32[]{:S(2)}) copy-start(bf16[64,4096]{1,0:T(8,128)(2,1)S(1)} %fusion.4) | copy-start | bytes 1572868
  143.8 15.0 %collective-permute-start.6 = (bf16[64,256]{1,0:T(8,128)(2,1)S(1)}, bf16[64,256]{1,0:T(8,128)(2,1)S(1)}, u32[]{:S(2)}, u32[]{:S(2)}) collective-permute-start(bf16[64,256]{1,0:T(8,128)(2,1)S(1)} %get-tuple-element.5), channel_id=1, source_target_pairs={{0,1},{2,3},{4,5},{6,7},{8,9},{10,11},{12,13},{14,15},{16,17},{18,... | collective-permute-start | bytes 98312 | tf_op jit(solution)/shard_map/ppermute | solution.py:20
  145.9 12.9 %collective-permute-start.7 = (bf16[64,256]{1,0:T(8,128)(2,1)S(1)}, bf16[64,256]{1,0:T(8,128)(2,1)S(1)}, u32[]{:S(2)}, u32[]{:S(2)}) collective-permute-start(bf16[64,256]{1,0:T(8,128)(2,1)S(1)} %get-tuple-element.6), channel_id=1, source_target_pairs={{1,0},{3,2},{5,4},{7,6},{9,8},{11,10},{13,12},{15,14},{17,16},{19,... | collective-permute-start | bytes 98312 | tf_op jit(solution)/shard_map/ppermute | solution.py:23
  149.0 5.7 %copy-start.5 = (f32[32,64,128,1]{2,1,3,0:T(8,128)S(1)}, f32[32,64,128,1]{2,1,3,0:T(8,128)}, u32[]{:S(2)}) copy-start(f32[32,64,128,1]{2,1,3,0:T(8,128)} %copy-done.4) | copy-start | bytes 3145732
  151.6 7.2 %copy-start.10 = (bf16[64,4096]{1,0:T(8,128)(2,1)S(1)}, bf16[64,4096]{1,0:T(8,128)(2,1)}, u32[]{:S(2)}) copy-start(bf16[64,4096]{1,0:T(8,128)(2,1)} %copy-done.9) | copy-start | bytes 1572868
  169.7 4.1 %copy-start.7 = (bf16[16,64,256]{2,1,0:T(8,128)(2,1)S(1)}, bf16[16,64,256]{2,1,0:T(8,128)(2,1)}, u32[]{:S(2)}) copy-start(bf16[16,64,256]{2,1,0:T(8,128)(2,1)} %copy-done.6) | copy-start | bytes 1572868
  169.7 4.1 %copy-start.8 = (f32[64,16,256]{2,1,0:T(8,128)S(1)}, f32[64,16,256]{2,1,0:T(8,128)}, u32[]{:S(2)}) copy-start(f32[64,16,256]{2,1,0:T(8,128)} %reshape.50) | copy-start | bytes 3145732
Sparse Core Ops, SparseCore 0:
  10.1 63.0 all-gather.1
where the time goes:
time: 204 us; the launch traced here: 203 us
  waiting for transfers between devices  86 us (42%)
  matrix products  33.6 us (16%)
  local copies, waits for them, and re-layouts  29.7 us (15%)
  blocking collectives  19 us (9%)
  starting transfers between devices  17.3 us (8%)
  between operations  13.7 us (7%)
  other arithmetic  3.9 us (2%)
    all_gather x1, waiting for transfers between devices, local(): lax.all_gather(rotation, 'vec', axis=1, tiled=True)  66 us
    dot_general x4, matrix products, apply_matrix(): jnp.einsum('rjab,krjb->kra', blocks, picked, preferred_element_type=jnp.f...  30.5 us
    all_to_all x1, blocking collectives, local(): lax.all_to_all(filtered, 'vec', split_axis=1, concat_axis=0, tiled=True)  19 us
    all_to_all x1, waiting for transfers between devices, local(): lax.all_to_all(rotated, 'vec', split_axis=0, concat_axis=1, tiled=True)  14 us
    gather x4, local copies, waits for them, and re-layouts, apply_matrix(): picked = stacked[:, offsets]  12.2 us
    reshape x4, local copies, waits for them, and re-layouts, apply_matrix(): return product.reshape(extended.shape[0], -1)  9.18 us
    ppermute x4, starting transfers between devices, with_halo(): lax.ppermute(lax.slice_in_dim(block, block.shape[dim] - width, None, axis...  7.49 us
    transpose x4, local copies, waits for them, and re-layouts, apply_matrix(): jnp.einsum('rjab,krjb->kra', blocks, picked, preferred_element_type=jnp.f...  6.33 us
  transfers between devices with their start and end apart: 10, of which 5 were waited for; matrix products, arithmetic and copies ran while one was open for 6% of the time, Pallas kernels for 0%

commit v1 on v0

v1 whole, which is shorter than its diff:
```python
import functools

import jax
import jax.numpy as jnp
from jax import lax
from jax.experimental import pallas as pl
from jax.experimental.pallas import tpu as pltpu
from jax.sharding import PartitionSpec as P

HB = 2
STEPS = 4
UNROLL = 4

centre = 0.3
half_width = 1.2

VMEM = pl.BlockSpec(memory_space=pltpu.VMEM)
SMEM = pl.BlockSpec(memory_space=pltpu.SMEM)


def step_kernel(first, last, count, place, offsets, held, low, high, blocks, *refs):
    if first:
        previous = current = held
        outs = refs
    else:
        current, previous = refs[:2]
        outs = refs[2:]
    outs, field = outs[:-1], outs[-1]
    rows, listed = blocks.shape[:2]
    field[HB : HB + rows] = held[...]
    if count == 2:
        received = low[...]
        nothing = jnp.zeros_like(received)
        field[:HB] = jnp.where(place[0] == 1, received, nothing)
        field[HB + rows :] = jnp.where(place[0] == 0, received, nothing)
    else:
        field[:HB] = low[...]
        field[HB + rows :] = high[...]
    operand = outs[0]

    def body(row, carry):
        picked = jnp.concatenate([field[offsets[row, j]] for j in range(listed)], axis=1)
        matrix = jnp.concatenate([blocks[row, j] for j in range(listed)], axis=1)
        product = lax.dot_general(
            picked, matrix, (((1,), (1,)), ((), ())), preferred_element_type=jnp.float32
        )
        if first:
            following = (product - centre * current[row].astype(jnp.float32)) / half_width
        else:
            following = (
                2.0 * (product - centre * current[row]) / half_width
                - previous[row].astype(jnp.float32)
            )
        operand[row] = following.astype(jnp.bfloat16)
        if not last:
            outs[1][row] = following
        return carry

    lax.fori_loop(0, rows, body, 0, unroll=UNROLL)
    if not last:
        if count == 2:
            start = jnp.where(place[0] == 0, rows - HB, 0)
            outs[2][...] = operand[pl.ds(start, HB)]
        else:
            outs[2][...] = operand[:HB]
            outs[3][...] = operand[rows - HB :]


def filter_step(turn, count, place, offsets, held, halo, blocks, state):
    first, last = turn == 0, turn == STEPS - 1
    rows, columns, width = held.shape
    edge = jax.ShapeDtypeStruct((HB, columns, width), jnp.bfloat16)
    out_shape = [jax.ShapeDtypeStruct(held.shape, jnp.bfloat16)]
    if not last:
        out_shape.append(jax.ShapeDtypeStruct(held.shape, jnp.float32))
        out_shape += [edge] if count == 2 else [edge, edge]
    flops = 2 * blocks.size * columns
    return pl.pallas_call(
        functools.partial(step_kernel, first, last, count),
        out_shape=out_shape,
        in_specs=[SMEM, SMEM] + [VMEM] * (4 + len(state)),
        out_specs=[VMEM] * len(out_shape),
        scratch_shapes=[pltpu.VMEM((rows + 2 * HB, columns, width), jnp.bfloat16)],
        compiler_params=pltpu.CompilerParams(vmem_limit_bytes=8 * 2**20),
        cost_estimate=pl.CostEstimate(
            flops=flops, bytes_accessed=2 * blocks.size, transcendentals=0
        ),
        name="filter_step",
    )(place, offsets, held, *halo, blocks, *state)


def exchange(count, edges):
    if count == 2:
        received = lax.ppermute(edges[0], "row", [(0, 1), (1, 0)])
        return received, received
    first, last = edges
    forward = [(i, i + 1) for i in range(count - 1)]
    backward = [(i + 1, i) for i in range(count - 1)]
    return lax.ppermute(last, "row", forward), lax.ppermute(first, "row", backward)


def filter_panel(held, blocks, column_blocks):
    count = lax.axis_size("row")
    place = lax.axis_index("row")
    rows = held.shape[0]
    offsets = column_blocks - (place * rows - HB)
    place = place.astype(jnp.int32)[None]
    if count == 2:
        edges = [lax.dynamic_slice_in_dim(held, jnp.where(place[0] == 0, rows - HB, 0), HB)]
    else:
        edges = [held[:HB], held[rows - HB :]]
    operand, state = held, ()
    older, newer = None, held
    for turn in range(STEPS):
        halo = exchange(count, edges)
        outs = filter_step(turn, count, place, offsets, operand, halo, blocks, state)
        operand = outs[0]
        if turn < STEPS - 1:
            edges = outs[2:]
            older, newer = newer, outs[1]
            state = (newer, older)
    return operand


def gather_rotation(shard):
    vec = lax.axis_size("vec")
    side = lax.rem(lax.axis_index("row"), 2)
    half = shard.shape[0] // 2
    held = lax.dynamic_slice_in_dim(shard, side * half, half)[None]
    bits = []
    bit = 1
    while bit < vec:
        bits.append(bit)
        bit *= 2
    for bit in reversed(bits):
        other = lax.ppermute(held, "vec", [(i, i ^ bit) for i in range(vec)])
        held = jnp.concatenate([held[:, None], other[:, None]], axis=1).reshape(
            (-1,) + held.shape[1:]
        )
    other = lax.ppermute(held, "row", [(i, i ^ 1) for i in range(lax.axis_size("row"))])
    return held, other


def rotate_kernel(place, filtered, own, other, out, turned):
    vec, groups, columns, width = filtered.shape
    me, side = place[0], place[1]
    for group in range(groups):
        turned[group * width : (group + 1) * width, :] = filtered[:, group].reshape(
            vec * columns, width
        ).T
    rows = turned[...]
    span = max(1, 256 // columns)
    for start in range(0, vec, span):
        pieces = []
        for index in range(start, start + span):
            slot = me ^ index
            mine, theirs = own[slot], other[slot]
            pieces.append(jnp.where(side == 0, mine, theirs))
            pieces.append(jnp.where(side == 0, theirs, mine))
        matrix = jnp.concatenate(pieces, axis=0)
        product = lax.dot_general(
            rows, matrix, (((1,), (1,)), ((), ())), preferred_element_type=jnp.float32
        )
        out[:, start * columns : (start + span) * columns] = product.astype(jnp.bfloat16)


def rotate(filtered, own, other):
    vec, groups, columns, width = filtered.shape
    place = jnp.stack([lax.axis_index("vec"), lax.rem(lax.axis_index("row"), 2)]).astype(jnp.int32)
    return pl.pallas_call(
        rotate_kernel,
        out_shape=jax.ShapeDtypeStruct((groups * width, vec * columns), jnp.bfloat16),
        in_specs=[SMEM, VMEM, VMEM, VMEM],
        out_specs=VMEM,
        scratch_shapes=[pltpu.VMEM((groups * width, vec * columns), jnp.bfloat16)],
        compiler_params=pltpu.CompilerParams(vmem_limit_bytes=16 * 2**20),
        name="rotate",
    )(place, filtered, own, other)


def local(vectors, rotation, blocks, column_blocks):
    vec = lax.axis_size("vec")
    own_rows = vectors[0]
    rows, total = own_rows.shape
    columns = total // vec
    width = blocks.shape[-1]
    lanes = min(rows, width)
    groups = rows // lanes
    part = width // lanes
    sent = jnp.transpose(own_rows.reshape(groups, lanes, vec, columns), (2, 0, 3, 1))
    got = lax.all_to_all(sent, "vec", split_axis=0, concat_axis=0, tiled=True)
    own, other = gather_rotation(jnp.transpose(rotation))
    held = got.reshape(-1, part, columns, lanes).swapaxes(1, 2).reshape(-1, columns, width)
    filtered = filter_panel(held, blocks, column_blocks)
    back = filtered.reshape(-1, columns, part, lanes).swapaxes(1, 2)
    back = back.reshape(vec, groups, columns, lanes)
    returned = lax.all_to_all(back, "vec", split_axis=0, concat_axis=0, tiled=True)
    return rotate(returned, own, other)[None]


def solution(mesh):
    placed = (P("row", "vec", None), P(None, "vec"), P("row", None, None, None), P("row", None))
    return jax.shard_map(
        local, mesh=mesh, in_specs=placed, out_specs=P("row", "vec", None), check_vma=False
    )
```

time: 204 us -> 91.5 us (0.45)
  waiting for transfers between devices: 86 us -> 41.6 us
  matrix products: 33.6 us -> 0 us
  local copies, waits for them, and re-layouts: 29.7 us -> 7.41 us
  Pallas kernels: 0 us -> 21.6 us
  blocking collectives: 19 us -> 0 us
  between operations: 13.7 us -> 0.14 us
  other arithmetic: 3.9 us -> 0.27 us
  starting transfers between devices: 17.3 us -> 20 us
    all_gather x1 -> x0, waiting for transfers between devices: 66 us -> none  [local(): lax.all_gather(rotation, 'vec', axis=1, tiled=True)]
    dot_general x5 -> x0, matrix products: 33.6 us -> none  [the longest x4 30.5 us: apply_matrix(): jnp.einsum('rjab,krjb->kra', blocks, picked, preferred_element_type=jnp.f...]
    pallas_call x0 -> x5, Pallas kernels: none -> 21.6 us  [the longest x4 19.5 us: filter_step(): pl.pallas_call(functools.partial(step_kernel, first, last, count), out_sh...]
    ppermute x8 -> x9, waiting for transfers between devices: 5.36 us -> 26.3 us  [the longest x4 22.6 us: gather_rotation(): other = lax.ppermute(held, 'vec', [(i, i ^ bit) for i in range(vec)])]
    all_to_all x1 -> x0, blocking collectives: 19 us -> none  [local(): lax.all_to_all(filtered, 'vec', split_axis=1, concat_axis=0, tiled=True)]
    gather x4 -> x0, local copies, waits for them, and re-layouts: 12.2 us -> none  [apply_matrix(): picked = stacked[:, offsets]]
    reshape x4 -> x0, local copies, waits for them, and re-layouts: 9.18 us -> none  [apply_matrix(): return product.reshape(extended.shape[0], -1)]
    all_to_all x1 -> x2, starting transfers between devices: 4.42 us -> 12.8 us  [the longest x1 8.34 us: local(): got = lax.all_to_all(sent, 'vec', split_axis=0, concat_axis=0, tiled=True)]
  transfers between devices with their start and end apart: 10 -> 11, of which waited for: 5 -> 8; matrix products, arithmetic and copies ran while one was open for 6% -> 2% of each run, Pallas kernels for 0% -> 21%
where the time goes in v1:
time: 91.5 us; the launch traced here: 91 us
  waiting for transfers between devices  41.6 us (45%)
  Pallas kernels  21.6 us (24%)
  starting transfers between devices  20 us (22%)
  local copies, waits for them, and re-layouts  7.41 us (8%)
    ppermute x4, waiting for transfers between devices, gather_rotation(): other = lax.ppermute(held, 'vec', [(i, i ^ bit) for i in range(vec)])  22.6 us
    pallas_call x4, Pallas kernels, filter_step(): pl.pallas_call(functools.partial(step_kernel, first, last, count), out_sh...  19.5 us
    all_to_all x1, waiting for transfers between devices, local(): lax.all_to_all(back, 'vec', split_axis=0, concat_axis=0, tiled=True)  15.3 us
    all_to_all x1, starting transfers between devices, local(): got = lax.all_to_all(sent, 'vec', split_axis=0, concat_axis=0, tiled=True)  8.34 us
    ppermute x4, starting transfers between devices, gather_rotation(): other = lax.ppermute(held, 'vec', [(i, i ^ bit) for i in range(vec)])  6.01 us
    unnamed x6, local copies, waits for them, and re-layouts  5.39 us
    all_to_all x1, starting transfers between devices, local(): lax.all_to_all(back, 'vec', split_axis=0, concat_axis=0, tiled=True)  4.48 us
    ppermute x4, waiting for transfers between devices, exchange(): received = lax.ppermute(edges[0], 'row', [(0, 1), (1, 0)])  3.71 us
  transfers between devices with their start and end apart: 11, of which 8 were waited for; matrix products, arithmetic and copies ran while one was open for 2% of the time, Pallas kernels for 21%

profile of v1, /device:TPU:0, one launch (start us, length us, event | category | flops | bytes accessed | tf_op | source)
XLA Modules:
  0.0 91.0 jit_solution(6255722971441799458)
XLA Ops:
  0.0 1.2 %copy.12 = bf16[1,256,1024]{1,2,0:T(8,128)(2,1)S(1)} copy(bf16[1,256,1024]{2,1,0:T(8,128)(2,1)} %param.4) | data formatting | bytes 1048576 | tf_op args[0]
  1.2 0.9 %reshape_squeeze.3 = bf16[2,128,16,64]{1,0,3,2:T(2,128)(2,1)} reshape(bf16[1,256,1024]{1,2,0:T(8,128)(2,1)S(1)} %copy.12) | data formatting | bytes 1048576 | tf_op jit(solution)/shard_map/reshape;squeeze | solution.py:190
  2.2 8.3 %all-to-all-start = ((bf16[16,2,64,128]{3,1,2,0:T(2,128)(2,1)}), bf16[16,2,64,128]{3,1,2,0:T(2,128)(2,1)S(1)}, u32[]{:S(2)}, u32[]{:S(2)}) async-start(bf16[16,2,64,128]{3,1,2,0:T(2,128)(2,1)} %bitcast.3), calls=%async_computation | async-start | bytes 1048576 | tf_op jit(solution)/shard_map/all_to_all | solution.py:191
  10.5 0.9 dynamic-slice_bitcast_fusion
  11.4 2.9 %collective-permute-start.4 = (bf16[1,32,1024]{2,1,0:T(8,128)(2,1)S(1)}, bf16[1,32,1024]{2,1,0:T(8,128)(2,1)S(1)}, u32[]{:S(2)}, u32[]{:S(2)}) collective-permute-start(bf16[1,32,1024]{2,1,0:T(8,128)(2,1)S(1)} %get-tuple-element.26), channel_id=1, source_target_pairs={{0,16},{2,18},{4,20},{6,22},{8,24},{10,26},{12,28},{14,30},{16,0},... | collective-permute-start | bytes 196616 | tf_op jit(solution)/shard_map/ppermute | solution.py:136
  14.3 13.5 %collective-permute-done.4 = bf16[1,32,1024]{2,1,0:T(8,128)(2,1)S(1)} collective-permute-done((bf16[1,32,1024]{2,1,0:T(8,128)(2,1)S(1)}, bf16[1,32,1024]{2,1,0:T(8,128)(2,1)S(1)}, u32[]{:S(2)}, u32[]{:S(2)}) %collective-permute-start.4) | collective-permute-done | bytes 65568 | tf_op jit(solution)/shard_map/ppermute | solution.py:136
  27.7 0.1 collective-permute-start.5
  27.8 5.0 %collective-permute-done.5 = bf16[2,32,1024]{2,1,0:T(8,128)(2,1)S(1)} collective-permute-done((bf16[2,32,1024]{2,1,0:T(8,128)(2,1)S(1)}, bf16[2,32,1024]{2,1,0:T(8,128)(2,1)S(1)}, u32[]{:S(2)}, u32[]{:S(2)}) %collective-permute-start.5) | collective-permute-done | bytes 131104 | tf_op jit(solution)/shard_map/ppermute | solution.py:136
  32.8 1.5 %collective-permute-start.6 = (bf16[4,32,1024]{2,1,0:T(8,128)(2,1)S(1)}, bf16[4,32,1024]{2,1,0:T(8,128)(2,1)S(1)}, u32[]{:S(2)}, u32[]{:S(2)}) collective-permute-start(bf16[4,32,1024]{2,1,0:T(8,128)(2,1)S(1)} %bitcast.38), channel_id=1, source_target_pairs={{0,4},{2,6},{4,0},{6,2},{8,12},{10,14},{12,8},{14,10},{16,20},{18,... | collective-permute-start | bytes 786440 | tf_op jit(solution)/shard_map/ppermute | solution.py:136
  34.3 0.8 copy.11
  35.1 4.1 %collective-permute-done.6 = bf16[4,32,1024]{2,1,0:T(8,128)(2,1)S(1)} collective-permute-done((bf16[4,32,1024]{2,1,0:T(8,128)(2,1)S(1)}, bf16[4,32,1024]{2,1,0:T(8,128)(2,1)S(1)}, u32[]{:S(2)}, u32[]{:S(2)}) %collective-permute-start.6) | collective-permute-done | bytes 262176 | tf_op jit(solution)/shard_map/ppermute | solution.py:136
  39.3 1.5 %collective-permute-start.7 = (bf16[8,32,1024]{2,1,0:T(8,128)(2,1)S(1)}, bf16[8,32,1024]{2,1,0:T(8,128)(2,1)S(1)}, u32[]{:S(2)}, u32[]{:S(2)}) collective-permute-start(bf16[8,32,1024]{2,1,0:T(8,128)(2,1)S(1)} %bitcast.36), channel_id=1, source_target_pairs={{0,2},{2,0},{4,6},{6,4},{8,10},{10,8},{12,14},{14,12},{16,18},{18,... | collective-permute-start | bytes 1572872 | tf_op jit(solution)/shard_map/ppermute | solution.py:136
  40.9 0.1 copy.13
  41.1 1.2 %collective-permute-done.low.high = bf16[2,64,128]{2,1,0:T(8,128)(2,1)S(1)} collective-permute-done((bf16[2,64,128]{2,1,0:T(8,128)(2,1)S(1)}, bf16[2,64,128]{2,1,0:T(8,128)(2,1)S(1)}, u32[]{:S(2)}, u32[]{:S(2)}) %collective-permute-start) | collective-permute-done | bytes 32800 | tf_op jit(solution)/shard_map/ppermute | solution.py:94
  42.3 3.4 %copy-done = bf16[32,8,128,128]{3,2,1,0:T(8,128)(2,1)S(1)} copy-done((bf16[32,8,128,128]{3,2,1,0:T(8,128)(2,1)S(1)}, bf16[32,8,128,128]{3,2,1,0:T(8,128)(2,1)}, u32[]{:S(2)}) %copy-start) | copy-done | bytes 8388632
  45.7 4.7 %filter_step.4 = (bf16[32,64,128]{2,1,0:T(8,128)(2,1)S(1)}, f32[32,64,128]{2,1,0:T(8,128)S(1)}, bf16[2,64,128]{2,1,0:T(8,128)(2,1)S(1)}) custom-call(s32[1]{0:T(128)} %bitcast.2.place, s32[32,8]{1,0:T(8,128)S(1)} %broadcast_subtract_fusion.offsets, bf16[32,64,128]{2,1,0:T(8,128)(2,1)S(1)} %bitcast.32, bf16[2,64,128]{2,1,0:T(8,128)(2,1)S(1)} %collective-permute-done.low.high, ...), custom_call_target="tpu_custom_call" | custom-call | flops 536870912 | bytes 8388608 | tf_op jit(solution)/shard_map/filter_step/pallas_call | solution.py:78
  50.4 0.2 collective-permute-start.1
  50.6 1.0 %collective-permute-done.1.low.high = bf16[2,64,128]{2,1,0:T(8,128)(2,1)S(1)} collective-permute-done((bf16[2,64,128]{2,1,0:T(8,128)(2,1)S(1)}, bf16[2,64,128]{2,1,0:T(8,128)(2,1)S(1)}, u32[]{:S(2)}, u32[]{:S(2)}) %collective-permute-start.1) | collective-permute-done | bytes 32800 | tf_op jit(solution)/shard_map/ppermute | solution.py:94
  51.6 4.7 %filter_step.5 = (bf16[32,64,128]{2,1,0:T(8,128)(2,1)S(1)}, f32[32,64,128]{2,1,0:T(8,128)S(1)}, bf16[2,64,128]{2,1,0:T(8,128)(2,1)S(1)}) custom-call(s32[1]{0:T(128)} %bitcast.2.place, s32[32,8]{1,0:T(8,128)S(1)} %broadcast_subtract_fusion.offsets, bf16[32,64,128]{2,1,0:T(8,128)(2,1)S(1)} %get-tuple-element.14.held, ...), custom_call_target="tpu_custom_call" | custom-call | flops 536870912 | bytes 8388608 | tf_op jit(solution)/shard_map/filter_step/pallas_call | solution.py:78
  56.3 0.2 collective-permute-start.2
  56.6 1.0 %collective-permute-done.2.low.high = bf16[2,64,128]{2,1,0:T(8,128)(2,1)S(1)} collective-permute-done((bf16[2,64,128]{2,1,0:T(8,128)(2,1)S(1)}, bf16[2,64,128]{2,1,0:T(8,128)(2,1)S(1)}, u32[]{:S(2)}, u32[]{:S(2)}) %collective-permute-start.2) | collective-permute-done | bytes 32800 | tf_op jit(solution)/shard_map/ppermute | solution.py:94
  57.6 4.7 %filter_step.6 = (bf16[32,64,128]{2,1,0:T(8,128)(2,1)S(1)}, f32[32,64,128]{2,1,0:T(8,128)S(1)}, bf16[2,64,128]{2,1,0:T(8,128)(2,1)S(1)}) custom-call(s32[1]{0:T(128)} %bitcast.2.place, s32[32,8]{1,0:T(8,128)S(1)} %broadcast_subtract_fusion.offsets, bf16[32,64,128]{2,1,0:T(8,128)(2,1)S(1)} %get-tuple-element.17.held, ...), custom_call_target="tpu_custom_call" | custom-call | flops 536870912 | bytes 8388608 | tf_op jit(solution)/shard_map/filter_step/pallas_call | solution.py:78
  62.3 0.2 collective-permute-start.3
  62.5 0.1 pad_maximum_fusion
  62.6 0.1 copy.17
  62.7 0.4 collective-permute-start.8
  63.1 0.4 collective-permute-done.3.low.high
  63.6 5.5 %filter_step.7 = bf16[32,64,128]{2,1,0:T(8,128)(2,1)} custom-call(s32[1]{0:T(128)} %bitcast.2.place, s32[32,8]{1,0:T(8,128)S(1)} %broadcast_subtract_fusion.offsets, bf16[32,64,128]{2,1,0:T(8,128)(2,1)S(1)} %get-tuple-element.20.held, bf16[2,64,128]{2,1,0:T(8,128)(2,1)S(1)} %collective-permute-done.3.low.high, ...), custom_call_target="tpu_custom_call" | custom-call | flops 536870912 | bytes 8388608 | tf_op jit(solution)/shard_map/filter_step/pallas_call | solution.py:78
  69.0 4.5 %all-to-all-start.1 = ((bf16[16,2,64,128]{3,2,1,0:T(8,128)(2,1)}), bf16[16,2,64,128]{3,2,1,0:T(8,128)(2,1)S(1)}, u32[]{:S(2)}, u32[]{:S(2)}) async-start(bf16[16,2,64,128]{3,2,1,0:T(8,128)(2,1)} %bitcast.5), calls=%async_computation.1 | async-start | bytes 1048576 | tf_op jit(solution)/shard_map/all_to_all | solution.py:197
  73.5 0.1 pad_add_fusion.place
  73.6 15.3 %all-to-all-done.1.filtered = bf16[16,2,64,128]{3,2,1,0:T(8,128)(2,1)S(1)} async-done(((bf16[16,2,64,128]{3,2,1,0:T(8,128)(2,1)}), bf16[16,2,64,128]{3,2,1,0:T(8,128)(2,1)S(1)}, u32[]{:S(2)}, u32[]{:S(2)}) %all-to-all-start.1) | async-done | bytes 524320 | tf_op jit(solution)/shard_map/all_to_all | solution.py:197
  89.0 2.1 %rotate.1 = bf16[256,1024]{1,0:T(8,128)(2,1)} custom-call(s32[2]{0:T(128)S(1)} %pad_add_fusion.place, bf16[16,2,64,128]{3,2,1,0:T(8,128)(2,1)S(1)} %all-to-all-done.1.filtered, bf16[16,32,1024]{2,1,0:T(8,128)(2,1)S(1)} %bitcast.35, bf16[16,32,1024]{2,1,0:T(8,128)(2,1)S(1)} %collective-permute-done.8.other), custom_call_target="tpu_custom_call" | custom-call | tf_op jit(solution)/shard_map/rotate/pallas_call | solution.py:170
  (13 shorter events, 0.2 us)
Async XLA Ops:
  2.2 38.7 %all-to-all-start = ((bf16[16,2,64,128]{3,1,2,0:T(2,128)(2,1)}), bf16[16,2,64,128]{3,1,2,0:T(2,128)(2,1)S(1)}, u32[]{:S(2)}, u32[]{:S(2)}) async-start(bf16[16,2,64,128]{3,1,2,0:T(2,128)(2,1)} %bitcast.3), calls=%async_computation | async-start | bytes 1048576 | tf_op jit(solution)/shard_map/all_to_all | solution.py:191
  11.4 16.3 %collective-permute-start.4 = (bf16[1,32,1024]{2,1,0:T(8,128)(2,1)S(1)}, bf16[1,32,1024]{2,1,0:T(8,128)(2,1)S(1)}, u32[]{:S(2)}, u32[]{:S(2)}) collective-permute-start(bf16[1,32,1024]{2,1,0:T(8,128)(2,1)S(1)} %get-tuple-element.26), channel_id=1, source_target_pairs={{0,16},{2,18},{4,20},{6,22},{8,24},{10,26},{12,28},{14,30},{16,0},... | collective-permute-start | bytes 196616 | tf_op jit(solution)/shard_map/ppermute | solution.py:136
  27.7 5.0 %collective-permute-start.5 = (bf16[2,32,1024]{2,1,0:T(8,128)(2,1)S(1)}, bf16[2,32,1024]{2,1,0:T(8,128)(2,1)S(1)}, u32[]{:S(2)}, u32[]{:S(2)}) collective-permute-start(bf16[2,32,1024]{2,1,0:T(8,128)(2,1)S(1)} %get-tuple-element.24), channel_id=1, source_target_pairs={{0,8},{2,10},{4,12},{6,14},{8,0},{10,2},{12,4},{14,6},{16,24},{18,... | collective-permute-start | bytes 393224 | tf_op jit(solution)/shard_map/ppermute | solution.py:136
  32.8 6.4 %collective-permute-start.6 = (bf16[4,32,1024]{2,1,0:T(8,128)(2,1)S(1)}, bf16[4,32,1024]{2,1,0:T(8,128)(2,1)S(1)}, u32[]{:S(2)}, u32[]{:S(2)}) collective-permute-start(bf16[4,32,1024]{2,1,0:T(8,128)(2,1)S(1)} %bitcast.38), channel_id=1, source_target_pairs={{0,4},{2,6},{4,0},{6,2},{8,12},{10,14},{12,8},{14,10},{16,20},{18,... | collective-permute-start | bytes 786440 | tf_op jit(solution)/shard_map/ppermute | solution.py:136
  39.3 23.2 %collective-permute-start.7 = (bf16[8,32,1024]{2,1,0:T(8,128)(2,1)S(1)}, bf16[8,32,1024]{2,1,0:T(8,128)(2,1)S(1)}, u32[]{:S(2)}, u32[]{:S(2)}) collective-permute-start(bf16[8,32,1024]{2,1,0:T(8,128)(2,1)S(1)} %bitcast.36), channel_id=1, source_target_pairs={{0,2},{2,0},{4,6},{6,4},{8,10},{10,8},{12,14},{14,12},{16,18},{18,... | collective-permute-start | bytes 1572872 | tf_op jit(solution)/shard_map/ppermute | solution.py:136
  41.0 1.3 %collective-permute-start = (bf16[2,64,128]{2,1,0:T(8,128)(2,1)S(1)}, bf16[2,64,128]{2,1,0:T(8,128)(2,1)S(1)}, u32[]{:S(2)}, u32[]{:S(2)}) collective-permute-start(bf16[2,64,128]{2,1,0:T(8,128)(2,1)S(1)} %constant_dynamic-slice_fusion), channel_id=1, source_target_pairs={{0,1},{1,0},{2,3},{3,2},{4,5},{5,4},{6,7},{7,6},{8,9},{9,8},{10,11... | collective-permute-start | bytes 98312 | tf_op jit(solution)/shard_map/ppermute | solution.py:94
  42.3 3.4 %copy-start = (bf16[32,8,128,128]{3,2,1,0:T(8,128)(2,1)S(1)}, bf16[32,8,128,128]{3,2,1,0:T(8,128)(2,1)}, u32[]{:S(2)}) copy-start(bf16[32,8,128,128]{3,2,1,0:T(8,128)(2,1)} %blocks.7) | copy-start | bytes 25165828
  45.7 6.0 %copy-start.1 = (bf16[32,8,128,128]{3,2,1,0:T(8,128)(2,1)S(1)}, bf16[32,8,128,128]{3,2,1,0:T(8,128)(2,1)}, u32[]{:S(2)}) copy-start(bf16[32,8,128,128]{3,2,1,0:T(8,128)(2,1)} %blocks.7) | copy-start | bytes 25165828
  50.4 1.3 %collective-permute-start.1 = (bf16[2,64,128]{2,1,0:T(8,128)(2,1)S(1)}, bf16[2,64,128]{2,1,0:T(8,128)(2,1)S(1)}, u32[]{:S(2)}, u32[]{:S(2)}) collective-permute-start(bf16[2,64,128]{2,1,0:T(8,128)(2,1)S(1)} %get-tuple-element.15), channel_id=1, source_target_pairs={{0,1},{1,0},{2,3},{3,2},{4,5},{5,4},{6,7},{7,6},{8,9},{9,8},{10,11... | collective-permute-start | bytes 98312 | tf_op jit(solution)/shard_map/ppermute | solution.py:94
  56.3 1.3 %collective-permute-start.2 = (bf16[2,64,128]{2,1,0:T(8,128)(2,1)S(1)}, bf16[2,64,128]{2,1,0:T(8,128)(2,1)S(1)}, u32[]{:S(2)}, u32[]{:S(2)}) collective-permute-start(bf16[2,64,128]{2,1,0:T(8,128)(2,1)S(1)} %get-tuple-element.18), channel_id=1, source_target_pairs={{0,1},{1,0},{2,3},{3,2},{4,5},{5,4},{6,7},{7,6},{8,9},{9,8},{10,11... | collective-permute-start | bytes 98312 | tf_op jit(solution)/shard_map/ppermute | solution.py:94
  62.3 1.3 %collective-permute-start.3 = (bf16[2,64,128]{2,1,0:T(8,128)(2,1)S(1)}, bf16[2,64,128]{2,1,0:T(8,128)(2,1)S(1)}, u32[]{:S(2)}, u32[]{:S(2)}) collective-permute-start(bf16[2,64,128]{2,1,0:T(8,128)(2,1)S(1)} %get-tuple-element.21), channel_id=1, source_target_pairs={{0,1},{1,0},{2,3},{3,2},{4,5},{5,4},{6,7},{7,6},{8,9},{9,8},{10,11... | collective-permute-start | bytes 98312 | tf_op jit(solution)/shard_map/ppermute | solution.py:94
  62.7 10.9 %collective-permute-start.8 = (bf16[16,32,1024]{2,1,0:T(8,128)(2,1)S(1)}, bf16[16,32,1024]{2,1,0:T(8,128)(2,1)S(1)}, u32[]{:S(2)}, u32[]{:S(2)}) collective-permute-start(bf16[16,32,1024]{2,1,0:T(8,128)(2,1)S(1)} %bitcast.34), channel_id=1, source_target_pairs={{0,1},{1,0},{2,3},{3,2},{4,5},{5,4},{6,7},{7,6},{8,9},{9,8},{10,11... | collective-permute-start | bytes 3145736 | tf_op jit(solution)/shard_map/ppermute | solution.py:140
  69.0 19.9 %all-to-all-start.1 = ((bf16[16,2,64,128]{3,2,1,0:T(8,128)(2,1)}), bf16[16,2,64,128]{3,2,1,0:T(8,128)(2,1)S(1)}, u32[]{:S(2)}, u32[]{:S(2)}) async-start(bf16[16,2,64,128]{3,2,1,0:T(8,128)(2,1)} %bitcast.5), calls=%async_computation.1 | async-start | bytes 1048576 | tf_op jit(solution)/shard_map/all_to_all | solution.py:197

commit v2 on v0

v2 whole, which is shorter than its diff:
```python
import functools

import jax
import jax.numpy as jnp
from jax import lax
from jax.experimental import pallas as pl
from jax.experimental.pallas import tpu as pltpu
from jax.sharding import PartitionSpec as P


HB = 2
STEPS = 4
UNROLL = 8
TURNED = 4
DIRECT = 2

centre = 0.3
half_width = 1.2

VMEM = pl.BlockSpec(memory_space=pltpu.VMEM)
SMEM = pl.BlockSpec(memory_space=pltpu.SMEM)
ANY = pl.BlockSpec(memory_space=pl.ANY)


def in_hbm(array):
    return pltpu.with_memory_space_constraint(array, pltpu.HBM)


def identity(size):
    rows = lax.broadcasted_iota(jnp.int32, (size, size), 0)
    columns = lax.broadcasted_iota(jnp.int32, (size, size), 1)
    return (rows == columns).astype(jnp.bfloat16)


def turned_by(unit, block):
    return lax.dot_general(
        unit, block, (((1,), (1,)), ((), ())), preferred_element_type=jnp.float32
    ).astype(jnp.bfloat16)


def prepare_kernel(place, vectors, shard, sent, half, landing, leaving, arrived):
    groups, vec, columns, lanes = leaving.shape
    rows = half.shape[1]
    fetch = [
        pltpu.make_async_copy(
            vectors.at[0, pl.ds(group * lanes, lanes)], landing.at[group], arrived.at[group]
        )
        for group in range(groups)
    ]
    pick = pltpu.make_async_copy(
        shard.at[pl.ds(pl.multiple_of(place[1] * rows, rows), rows)],
        half.at[0],
        arrived.at[groups],
    )
    for copy in fetch:
        copy.start()
    pick.start()
    span = max(1, 256 // columns)
    unit = identity(span * columns)
    for group in range(groups):
        fetch[group].wait()
        for start in range(0, vec, span):
            piece = landing[group, :, start * columns : (start + span) * columns]
            leaving[group, start : start + span] = turned_by(unit, piece).reshape(
                span, columns, lanes
            )
        fetch[group] = pltpu.make_async_copy(
            leaving.at[group], sent.at[:, group], arrived.at[group]
        )
        fetch[group].start()
    pick.wait()
    for copy in fetch:
        copy.wait()


def prepare(place, vectors, shard, groups, lanes):
    columns, total = shard.shape
    return pl.pallas_call(
        prepare_kernel,
        out_shape=(
            pltpu.HBM((total // columns, groups, columns, lanes), jnp.bfloat16),
            jax.ShapeDtypeStruct((1, columns // 2, total), jnp.bfloat16),
        ),
        in_specs=[SMEM, ANY, ANY],
        out_specs=(ANY, VMEM),
        scratch_shapes=[
            pltpu.VMEM((groups, lanes, total), jnp.bfloat16),
            pltpu.VMEM((groups, total // columns, columns, lanes), jnp.bfloat16),
            pltpu.SemaphoreType.DMA((groups + 1,)),
        ],
        compiler_params=pltpu.CompilerParams(vmem_limit_bytes=8 * 2**20),
        name="prepare",
    )(place, in_hbm(vectors), in_hbm(shard))


def turn_kernel(blocks, turned):
    rows, listed, width = blocks.shape[:3]
    unit = identity(2 * width)
    for row in range(rows):
        for j in range(0, listed, 2):
            pair = jnp.concatenate([blocks[row, j], blocks[row, j + 1]], axis=1)
            turned[row, j * width : (j + 2) * width, :] = turned_by(unit, pair)


def turn_blocks(blocks, first, rows):
    listed, width = blocks.shape[1:3]
    skipped = first // TURNED
    size = rows * listed * width * width
    return pl.pallas_call(
        turn_kernel,
        grid=(rows // TURNED,),
        out_shape=pltpu.HBM((rows, listed * width, width), jnp.bfloat16),
        in_specs=[
            pl.BlockSpec((TURNED, listed, width, width), lambda row: (row + skipped, 0, 0, 0))
        ],
        out_specs=pl.BlockSpec((TURNED, listed * width, width), lambda row: (row, 0, 0)),
        compiler_params=pltpu.CompilerParams(vmem_limit_bytes=16 * 2**20),
        cost_estimate=pl.CostEstimate(
            flops=4 * width * size, bytes_accessed=4 * size, transcendentals=0
        ),
        name="turn_blocks",
    )(in_hbm(blocks))


def load_kernel(source, out, arrived):
    copy = pltpu.make_async_copy(source, out, arrived)
    copy.start()
    copy.wait()


def load_head(head):
    return pl.pallas_call(
        load_kernel,
        out_shape=jax.ShapeDtypeStruct(head.shape, head.dtype),
        in_specs=[ANY],
        out_specs=VMEM,
        scratch_shapes=[pltpu.SemaphoreType.DMA],
        compiler_params=pltpu.CompilerParams(vmem_limit_bytes=4 * 2**20),
        cost_estimate=pl.CostEstimate(
            flops=0, bytes_accessed=2 * head.size, transcendentals=0
        ),
        name="load_head",
    )(in_hbm(head))


def step_kernel(first, last, count, place, listing, held, low, high, head, tail, *refs):
    refs = list(refs)
    moved = refs.pop()
    field = refs.pop()
    if first:
        source, tail = tail, refs.pop()

        def load(chunk):
            return pltpu.make_async_copy(
                source.at[pl.ds(chunk * UNROLL, UNROLL)],
                tail.at[pl.ds(chunk * UNROLL, UNROLL)],
                moved.at[chunk],
            )

        for chunk in range(tail.shape[0] // UNROLL):
            load(chunk).start()
        previous = current = held
    else:
        current, previous = refs[:2]
        refs = refs[2:]
    if last:
        result, operand = refs

        def store(chunk):
            some = pl.ds(chunk * UNROLL, UNROLL)
            return pltpu.make_async_copy(operand.at[some], result.at[some], moved.at[chunk])

    else:
        operand = refs[0]
    listed, rows = listing.shape
    shift = place[0] * rows - HB
    field[HB : HB + rows] = held[...]
    if count == 2:
        received = low[...]
        nothing = jnp.zeros_like(received)
        field[:HB] = jnp.where(place[0] == 1, received, nothing)
        field[HB + rows :] = jnp.where(place[0] == 0, received, nothing)
    else:
        field[:HB] = low[...]
        field[HB + rows :] = high[...]

    def one(row, matrix):
        picked = jnp.concatenate(
            [field[listing[j, row] - shift] for j in range(listed)], axis=1
        )
        product = jnp.dot(picked, matrix, preferred_element_type=jnp.float32)
        if first:
            following = (product - centre * current[row].astype(jnp.float32)) / half_width
        else:
            following = (
                2.0 * (product - centre * current[row]) / half_width
                - previous[row].astype(jnp.float32)
            )
        operand[row] = following.astype(jnp.bfloat16)
        if not last:
            refs[1][row] = following

    for row in range(UNROLL):
        one(row, head[row])
    if last:
        store(0).start()

    def body(chunk, carry):
        if first:
            load(chunk - 1).wait()
        for index in range(UNROLL):
            one(chunk * UNROLL + index, tail[(chunk - 1) * UNROLL + index])
        if last:
            store(chunk).start()
        return carry

    lax.fori_loop(1, rows // UNROLL, body, 0)
    if last:
        for chunk in range(rows // UNROLL):
            store(chunk).wait()
    elif count == 2:
        start = jnp.where(place[0] == 0, rows - HB, 0)
        refs[2][...] = operand[pl.ds(start, HB)]
    else:
        refs[2][...] = operand[:HB]
        refs[3][...] = operand[rows - HB :]


def filter_step(turn, count, place, listing, held, halo, head, tail, state):
    first, last = turn == 0, turn == STEPS - 1
    rows, columns, width = held.shape
    edge = jax.ShapeDtypeStruct((HB, columns, width), jnp.bfloat16)
    args = [place, listing, held, *halo, head, in_hbm(tail) if first else tail, *state]
    in_specs = [SMEM, SMEM] + [VMEM] * (len(args) - 2)
    scratch = [pltpu.VMEM((rows + 2 * HB, columns, width), jnp.bfloat16)]
    if last:
        out_shape = [pltpu.HBM(held.shape, jnp.bfloat16)]
        out_specs = [ANY]
        scratch = [pltpu.VMEM(held.shape, jnp.bfloat16)] + scratch
    else:
        out_shape = [
            jax.ShapeDtypeStruct(held.shape, jnp.bfloat16),
            jax.ShapeDtypeStruct(held.shape, jnp.float32),
        ]
        out_shape += [edge] if count == 2 else [edge, edge]
        if first:
            in_specs[6] = ANY
            out_shape.append(jax.ShapeDtypeStruct(tail.shape, tail.dtype))
        out_specs = [VMEM] * len(out_shape)
    scratch.append(pltpu.SemaphoreType.DMA((rows // UNROLL,)))
    size = tail.size
    return pl.pallas_call(
        functools.partial(step_kernel, first, last, count),
        out_shape=out_shape,
        in_specs=in_specs,
        out_specs=out_specs,
        scratch_shapes=scratch,
        compiler_params=pltpu.CompilerParams(vmem_limit_bytes=8 * 2**20),
        cost_estimate=pl.CostEstimate(
            flops=2 * size * columns, bytes_accessed=2 * size, transcendentals=0
        ),
        name="filter_step",
    )(*args)


def join_kernel(*refs):
    out = refs[-1]
    for index in range(out.shape[0]):
        out[index : index + 1] = refs[index][...]


def join(pieces, after):
    return pl.pallas_call(
        join_kernel,
        out_shape=jax.ShapeDtypeStruct((len(pieces),) + pieces[0].shape[1:], jnp.bfloat16),
        in_specs=[VMEM] * len(pieces) + [ANY],
        out_specs=VMEM,
        compiler_params=pltpu.CompilerParams(vmem_limit_bytes=2 * 2**20),
        name="join",
    )(*pieces, after)


def exchange(count, edges):
    if count == 2:
        received = lax.ppermute(edges[0], "row", [(0, 1), (1, 0)])
        return received, received
    first, last = edges
    forward = [(i, i + 1) for i in range(count - 1)]
    backward = [(i + 1, i) for i in range(count - 1)]
    return lax.ppermute(last, "row", forward), lax.ppermute(first, "row", backward)


def meet(array, code):
    pairs = [(i, i ^ code) for i in range(lax.axis_size("vec"))]
    return lax.ppermute(array, "vec", pairs)


def assemble_kernel(low, place, *refs):
    parts = 1 << low
    shards = refs[: 2 * parts]
    out, ordered = refs[2 * parts :]
    vec, _, half, total = ordered.shape
    side, me = place[1], place[2]
    for index in range(2 * parts):
        owner, part = index // parts, index % parts
        for slot in range(vec // parts):
            ordered[me ^ (slot << low | part), side ^ owner] = shards[index][slot]
    columns = 2 * half
    span = max(1, 256 // columns)
    wide = span * columns
    unit = identity(wide)
    for start in range(0, vec, span):
        rows = ordered[start : start + span].reshape(wide, total)
        for left in range(0, total, wide):
            out[left : left + wide, start * columns : (start + span) * columns] = turned_by(
                unit, rows[:, left : left + wide]
            )


def assemble(place, mine, theirs):
    parts = len(mine)
    slots, half, total = mine[0].shape
    return pl.pallas_call(
        functools.partial(assemble_kernel, parts.bit_length() - 1),
        out_shape=jax.ShapeDtypeStruct((total, total), jnp.bfloat16),
        in_specs=[SMEM] + [VMEM] * (2 * parts),
        out_specs=VMEM,
        scratch_shapes=[pltpu.VMEM((parts * slots, 2, half, total), jnp.bfloat16)],
        compiler_params=pltpu.CompilerParams(vmem_limit_bytes=8 * 2**20),
        cost_estimate=pl.CostEstimate(
            flops=512 * total * total, bytes_accessed=4 * total * total, transcendentals=0
        ),
        name="assemble",
    )(place, *mine, *theirs)


def rotate_kernel(filtered, rotation, out, rows, leaving, sent):
    _, groups, _, width = filtered.shape
    total = rotation.shape[0]
    wide = leaving.shape[2]
    unit = identity(width)
    for group in range(groups):
        turned = filtered[:, group].reshape(total, width)
        for start in range(0, total, wide):
            rows[group * width : (group + 1) * width, start : start + wide] = turned_by(
                unit, turned[start : start + wide]
            )
    copies = []
    for chunk in range(total // wide):
        some = slice(chunk * wide, (chunk + 1) * wide)
        leaving[chunk] = jnp.dot(
            rows[...], rotation[:, some], preferred_element_type=jnp.float32
        ).astype(jnp.bfloat16)
        copies.append(pltpu.make_async_copy(leaving.at[chunk], out.at[:, some], sent.at[chunk]))
        copies[-1].start()
    for copy in copies:
        copy.wait()


def rotate(filtered, rotation):
    vec, groups, columns, width = filtered.shape
    rows, total = groups * width, vec * columns
    wide = min(256, total)
    return pl.pallas_call(
        rotate_kernel,
        out_shape=pltpu.HBM((rows, total), jnp.bfloat16),
        in_specs=[VMEM, VMEM],
        out_specs=ANY,
        scratch_shapes=[
            pltpu.VMEM((rows, total), jnp.bfloat16),
            pltpu.VMEM((total // wide, rows, wide), jnp.bfloat16),
            pltpu.SemaphoreType.DMA((total // wide,)),
        ],
        compiler_params=pltpu.CompilerParams(vmem_limit_bytes=16 * 2**20),
        name="rotate",
    )(filtered, rotation)


def local(vectors, rotation, blocks, column_blocks):
    vec, count = lax.axis_size("vec"), lax.axis_size("row")
    rows, total = vectors.shape[1:]
    columns = total // vec
    width = blocks.shape[-1]
    lanes = min(rows, width)
    groups = rows // lanes
    part = width // lanes
    row = lax.axis_index("row")
    place = jnp.stack([row, row & 1, lax.axis_index("vec")]).astype(jnp.int32)
    listing = jnp.transpose(column_blocks)
    bits = vec.bit_length() - 1
    low = max(0, bits - DIRECT)

    sent, half = prepare(place, vectors, jnp.transpose(rotation), groups, lanes)
    got = lax.all_to_all(sent, "vec", split_axis=0, concat_axis=0, tiled=True)
    pieces = [half]
    for code in range(1, vec >> low):
        pieces.append(meet(half, code << low))
    tail = turn_blocks(blocks, UNROLL, blocks.shape[0] - UNROLL)
    head = turn_blocks(blocks, 0, UNROLL)
    held = got.reshape(-1, part, columns, lanes).swapaxes(1, 2).reshape(-1, columns, width)

    if count == 2:
        start = jnp.where(row == 0, held.shape[0] - HB, 0)
        edges = [lax.dynamic_slice_in_dim(held, start, HB)]
    else:
        edges = [held[:HB], held[held.shape[0] - HB :]]
    operand, state = held, ()
    older, newer = None, held
    head = load_head(head)
    for turn in range(STEPS):
        halo = exchange(count, edges)
        outs = filter_step(turn, count, place, listing, operand, halo, head, tail, state)
        operand = outs[0]
        if turn == 0:
            outs, tail = outs[:-1], outs[-1]
            mine = [join(pieces, outs[2])]
        if turn < STEPS - 1:
            edges = outs[2 : 3 if count == 2 else 4]
            older, newer = newer, outs[1]
            state = (newer, older)
    for bit in range(low):
        more = []
        for array in mine:
            more.append(meet(array, 1 << bit))
        mine += more

    back = operand.reshape(-1, columns, part, lanes).swapaxes(1, 2)
    back = back.reshape(vec, groups, columns, lanes)
    returned = lax.all_to_all(back, "vec", split_axis=0, concat_axis=0, tiled=True)
    theirs = []
    for array in mine:
        theirs.append(lax.ppermute(array, "row", [(i, i ^ 1) for i in range(count)]))
    rotation = assemble(place, mine, theirs)
    return rotate(returned, rotation)[None]


def solution(mesh):
    placed = (P("row", "vec", None), P(None, "vec"), P("row", None, None, None), P("row", None))

    return jax.shard_map(
        local, mesh=mesh, in_specs=placed, out_specs=P("row", "vec", None), check_vma=False
    )
```

time: 204 us -> 91.8 us (0.45)
  waiting for transfers between devices: 86 us -> 34.7 us
  matrix products: 33.6 us -> 0 us
  Pallas kernels: 0 us -> 33.2 us
  local copies, waits for them, and re-layouts: 29.7 us -> 0.01 us
  blocking collectives: 19 us -> 0 us
  between operations: 13.7 us -> 0.14 us
  starting transfers between devices: 17.3 us -> 23.1 us
  other arithmetic: 3.9 us -> 0.08 us
    all_gather x1 -> x0, waiting for transfers between devices: 66 us -> none  [local(): lax.all_gather(rotation, 'vec', axis=1, tiled=True)]
    dot_general x5 -> x0, matrix products: 33.6 us -> none  [the longest x4 30.5 us: apply_matrix(): jnp.einsum('rjab,krjb->kra', blocks, picked, preferred_element_type=jnp.f...]
    pallas_call x0 -> x11, Pallas kernels: none -> 33.2 us  [the longest x4 13.6 us: filter_step(): pl.pallas_call(functools.partial(step_kernel, first, last, count), out_sh...]
    ppermute x8 -> x14, waiting for transfers between devices: 5.36 us -> 28 us  [the longest x6 23.9 us: meet(): return lax.ppermute(array, 'vec', pairs)]
    all_to_all x1 -> x0, blocking collectives: 19 us -> none  [local(): lax.all_to_all(filtered, 'vec', split_axis=1, concat_axis=0, tiled=True)]
    gather x4 -> x0, local copies, waits for them, and re-layouts: 12.2 us -> none  [apply_matrix(): picked = stacked[:, offsets]]
    reshape x4 -> x0, local copies, waits for them, and re-layouts: 9.18 us -> none  [apply_matrix(): return product.reshape(extended.shape[0], -1)]
    all_to_all x1 -> x2, starting transfers between devices: 4.42 us -> 12.3 us  [the longest x1 8.34 us: local(): got = lax.all_to_all(sent, 'vec', split_axis=0, concat_axis=0, tiled=True)]
  transfers between devices with their start and end apart: 10 -> 16, of which waited for: 5 -> 10; matrix products, arithmetic and copies ran while one was open for 6% -> 0% of each run, Pallas kernels for 0% -> 17%
where the time goes in v2:
time: 91.8 us; the launch traced here: 91.2 us
  waiting for transfers between devices  34.7 us (38%)
  Pallas kernels  33.2 us (36%)
  starting transfers between devices  23.1 us (25%)
    ppermute x6, waiting for transfers between devices, meet(): return lax.ppermute(array, 'vec', pairs)  23.9 us
    pallas_call x4, Pallas kernels, filter_step(): pl.pallas_call(functools.partial(step_kernel, first, last, count), out_sh...  13.6 us
    pallas_call x2, Pallas kernels, turn_blocks(): pl.pallas_call(turn_kernel, grid=(rows // TURNED,), out_shape=pltpu.HBM((...  12.2 us
    ppermute x6, starting transfers between devices, meet(): return lax.ppermute(array, 'vec', pairs)  8.91 us
    all_to_all x1, starting transfers between devices, local(): got = lax.all_to_all(sent, 'vec', split_axis=0, concat_axis=0, tiled=True)  8.34 us
    all_to_all x1, waiting for transfers between devices, local(): got = lax.all_to_all(sent, 'vec', split_axis=0, concat_axis=0, tiled=True)  6.64 us
    all_to_all x1, starting transfers between devices, local(): lax.all_to_all(back, 'vec', split_axis=0, concat_axis=0, tiled=True)  3.96 us
    pallas_call x1, Pallas kernels, prepare(): pl.pallas_call(prepare_kernel, out_shape=(pltpu.HBM((total // columns, gr...  2.82 us
  transfers between devices with their start and end apart: 16, of which 10 were waited for; matrix products, arithmetic and copies ran while one was open for 0% of the time, Pallas kernels for 17%

profile of v2, /device:TPU:0, one launch (start us, length us, event | category | flops | bytes accessed | tf_op | source)
XLA Modules:
  0.0 91.2 jit_solution(8454965639417369809)
XLA Ops:
  0.1 2.8 %prepare.1 = (bf16[16,2,64,128]{3,2,1,0:T(8,128)(2,1)}, bf16[1,32,1024]{2,1,0:T(8,128)(2,1)S(1)}) custom-call(s32[3]{0:T(128)S(1)} %pad_add_fusion.place, bf16[1,256,1024]{2,1,0:T(8,128)(2,1)} %vectors.1, bf16[64,1024]{1,0:T(8,128)(2,1)} %bitcast.16), custom_call_target="tpu_custom_call" | custom-call | tf_op jit(solution)/shard_map/prepare/pallas_call | solution.py:78
  2.9 8.3 %all-to-all-start = ((bf16[16,2,64,128]{3,2,1,0:T(8,128)(2,1)}), bf16[16,2,64,128]{3,2,1,0:T(8,128)(2,1)S(1)}, u32[]{:S(2)}, u32[]{:S(2)}) async-start(bf16[16,2,64,128]{3,2,1,0:T(8,128)(2,1)} %get-tuple-element.17), calls=%async_computation | async-start | bytes 1048576 | tf_op jit(solution)/shard_map/all_to_all | solution.py:394
  11.3 8.4 %turn_blocks.3.tail = bf16[24,1024,128]{2,1,0:T(8,128)(2,1)} custom-call(bf16[32,8,128,128]{3,2,1,0:T(8,128)(2,1)} %blocks.3), custom_call_target="tpu_custom_call" | custom-call | flops 1610612736 | bytes 12582912 | tf_op jit(solution)/shard_map/turn_blocks/pallas_call | solution.py:109
  19.7 6.6 %all-to-all-done = bf16[16,2,64,128]{3,2,1,0:T(8,128)(2,1)S(1)} async-done(((bf16[16,2,64,128]{3,2,1,0:T(8,128)(2,1)}), bf16[16,2,64,128]{3,2,1,0:T(8,128)(2,1)S(1)}, u32[]{:S(2)}, u32[]{:S(2)}) %all-to-all-start) | async-done | bytes 524320 | tf_op jit(solution)/shard_map/all_to_all | solution.py:394
  26.4 3.7 %turn_blocks.2.source = bf16[8,1024,128]{2,1,0:T(8,128)(2,1)} custom-call(bf16[32,8,128,128]{3,2,1,0:T(8,128)(2,1)} %blocks.3), custom_call_target="tpu_custom_call" | custom-call | flops 536870912 | bytes 4194304 | tf_op jit(solution)/shard_map/turn_blocks/pallas_call | solution.py:109
  30.1 1.6 %load_head.1.head = bf16[8,1024,128]{2,1,0:T(8,128)(2,1)S(1)} custom-call(bf16[8,1024,128]{2,1,0:T(8,128)(2,1)} %turn_blocks.2.source), custom_call_target="tpu_custom_call" | custom-call | bytes 2097152 | tf_op jit(solution)/shard_map/load_head/pallas_call | solution.py:132
  31.7 4.4 %filter_step.4 = (bf16[32,64,128]{2,1,0:T(8,128)(2,1)S(1)}, f32[32,64,128]{2,1,0:T(8,128)S(1)}, bf16[2,64,128]{2,1,0:T(8,128)(2,1)S(1)}, bf16[24,1024,128]{2,1,0:T(8,128)(2,1)S(1)}) custom-call(s32[3]{0:T(128)S(1)} %pad_add_fusion.place, s32[8,32]{1,0:T(8,128)S(1)} %bitcast.11, bf16[32,64,128]{2,1,0:T(8,128)(2,1)S(1)} %bitcast.9, ...), custom_call_target="tpu_custom_call" | custom-call | flops 402653184 | bytes 6291456 | tf_op jit(solution)/shard_map/filter_step/pallas_call | solution.py:252
  36.1 0.6 collective-permute-start.1
  36.7 0.9 collective-permute-done.1.low.high
  37.5 2.9 %filter_step.5 = (bf16[32,64,128]{2,1,0:T(8,128)(2,1)S(1)}, f32[32,64,128]{2,1,0:T(8,128)S(1)}, bf16[2,64,128]{2,1,0:T(8,128)(2,1)S(1)}) custom-call(s32[3]{0:T(128)S(1)} %pad_add_fusion.place, s32[8,32]{1,0:T(8,128)S(1)} %bitcast.12, bf16[32,64,128]{2,1,0:T(8,128)(2,1)S(1)} %get-tuple-element.18.held, ...), custom_call_target="tpu_custom_call" | custom-call | flops 402653184 | bytes 6291456 | tf_op jit(solution)/shard_map/filter_step/pallas_call | solution.py:252
  40.4 0.4 collective-permute-start.2
  40.8 0.9 collective-permute-done.2.low.high
  41.7 2.8 %filter_step.6 = (bf16[32,64,128]{2,1,0:T(8,128)(2,1)S(1)}, f32[32,64,128]{2,1,0:T(8,128)S(1)}, bf16[2,64,128]{2,1,0:T(8,128)(2,1)S(1)}) custom-call(s32[3]{0:T(128)S(1)} %pad_add_fusion.place, s32[8,32]{1,0:T(8,128)S(1)} %bitcast.13, bf16[32,64,128]{2,1,0:T(8,128)(2,1)S(1)} %get-tuple-element.22.held, ...), custom_call_target="tpu_custom_call" | custom-call | flops 402653184 | bytes 6291456 | tf_op jit(solution)/shard_map/filter_step/pallas_call | solution.py:252
  44.5 0.4 collective-permute-start.3
  44.9 0.9 collective-permute-done.3.low.high
  45.8 3.5 %filter_step.7 = bf16[32,64,128]{2,1,0:T(8,128)(2,1)} custom-call(s32[3]{0:T(128)S(1)} %pad_add_fusion.place, s32[8,32]{1,0:T(8,128)S(1)} %bitcast.14, bf16[32,64,128]{2,1,0:T(8,128)(2,1)S(1)} %get-tuple-element.25.held, bf16[2,64,128]{2,1,0:T(8,128)(2,1)S(1)} %collective-permute-done.3.low.high, bf16[2,64,128]{2,1,0:T(8,128)(2,1)S(1)} %collective-permute-done.3.low.high, ...), custom_call_target="tpu_custom_call" | custom-call | flops 402653184 | bytes 6291456 | tf_op jit(solution)/shard_map/filter_step/pallas_call | solution.py:252
  49.3 4.0 %all-to-all-start.1 = ((bf16[16,2,64,128]{3,2,1,0:T(8,128)(2,1)}), bf16[16,2,64,128]{3,2,1,0:T(8,128)(2,1)S(1)}, u32[]{:S(2)}, u32[]{:S(2)}) async-start(bf16[16,2,64,128]{3,2,1,0:T(8,128)(2,1)} %bitcast.15), calls=%async_computation.1 | async-start | bytes 1048576 | tf_op jit(solution)/shard_map/all_to_all | solution.py:429
  53.3 1.9 %collective-permute-start.4 = (bf16[1,32,1024]{2,1,0:T(8,128)(2,1)S(1)}, bf16[1,32,1024]{2,1,0:T(8,128)(2,1)S(1)}, u32[]{:S(2)}, u32[]{:S(2)}) collective-permute-start(bf16[1,32,1024]{2,1,0:T(8,128)(2,1)S(1)} %get-tuple-element.28.refs_0_), channel_id=1, source_target_pairs={{0,8},{2,10},{4,12},{6,14},{8,0},{10,2},{12,4},{14,6},{16,24},{18,... | collective-permute-start | bytes 196616 | tf_op jit(solution)/shard_map/ppermute | solution.py:295
  55.2 2.4 %collective-permute-start.5 = (bf16[1,32,1024]{2,1,0:T(8,128)(2,1)S(1)}, bf16[1,32,1024]{2,1,0:T(8,128)(2,1)S(1)}, u32[]{:S(2)}, u32[]{:S(2)}) collective-permute-start(bf16[1,32,1024]{2,1,0:T(8,128)(2,1)S(1)} %get-tuple-element.28.refs_0_), channel_id=1, source_target_pairs={{0,16},{2,18},{4,20},{6,22},{8,24},{10,26},{12,28},{14,30},{16,0},... | collective-permute-start | bytes 196616 | tf_op jit(solution)/shard_map/ppermute | solution.py:295
  57.6 0.2 collective-permute-start.6
  57.7 7.2 %collective-permute-done.4.refs_1_ = bf16[1,32,1024]{2,1,0:T(8,128)(2,1)S(1)} collective-permute-done((bf16[1,32,1024]{2,1,0:T(8,128)(2,1)S(1)}, bf16[1,32,1024]{2,1,0:T(8,128)(2,1)S(1)}, u32[]{:S(2)}, u32[]{:S(2)}) %collective-permute-start.4) | collective-permute-done | bytes 65568 | tf_op jit(solution)/shard_map/ppermute | solution.py:295
  64.9 8.2 %collective-permute-done.5.refs_2_ = bf16[1,32,1024]{2,1,0:T(8,128)(2,1)S(1)} collective-permute-done((bf16[1,32,1024]{2,1,0:T(8,128)(2,1)S(1)}, bf16[1,32,1024]{2,1,0:T(8,128)(2,1)S(1)}, u32[]{:S(2)}, u32[]{:S(2)}) %collective-permute-start.5) | collective-permute-done | bytes 65568 | tf_op jit(solution)/shard_map/ppermute | solution.py:295
  73.1 1.5 %collective-permute-start.7 = (bf16[4,32,1024]{2,1,0:T(8,128)(2,1)S(1)}, bf16[4,32,1024]{2,1,0:T(8,128)(2,1)S(1)}, u32[]{:S(2)}, u32[]{:S(2)}) collective-permute-start(bf16[4,32,1024]{2,1,0:T(8,128)(2,1)S(1)} %join.1.refs_0_), channel_id=1, source_target_pairs={{0,2},{2,0},{4,6},{6,4},{8,10},{10,8},{12,14},{14,12},{16,18},{18,... | collective-permute-start | bytes 786440 | tf_op jit(solution)/shard_map/ppermute | solution.py:295
  74.6 1.5 %collective-permute-start.8 = (bf16[4,32,1024]{2,1,0:T(8,128)(2,1)S(1)}, bf16[4,32,1024]{2,1,0:T(8,128)(2,1)S(1)}, u32[]{:S(2)}, u32[]{:S(2)}) collective-permute-start(bf16[4,32,1024]{2,1,0:T(8,128)(2,1)S(1)} %join.1.refs_0_), channel_id=1, source_target_pairs={{0,4},{2,6},{4,0},{6,2},{8,12},{10,14},{12,8},{14,10},{16,20},{18,... | collective-permute-start | bytes 786440 | tf_op jit(solution)/shard_map/ppermute | solution.py:295
  76.1 3.5 %collective-permute-done.7.refs_1_ = bf16[4,32,1024]{2,1,0:T(8,128)(2,1)S(1)} collective-permute-done((bf16[4,32,1024]{2,1,0:T(8,128)(2,1)S(1)}, bf16[4,32,1024]{2,1,0:T(8,128)(2,1)S(1)}, u32[]{:S(2)}, u32[]{:S(2)}) %collective-permute-start.7) | collective-permute-done | bytes 262176 | tf_op jit(solution)/shard_map/ppermute | solution.py:295
  79.6 1.5 %collective-permute-start.9 = (bf16[4,32,1024]{2,1,0:T(8,128)(2,1)S(1)}, bf16[4,32,1024]{2,1,0:T(8,128)(2,1)S(1)}, u32[]{:S(2)}, u32[]{:S(2)}) collective-permute-start(bf16[4,32,1024]{2,1,0:T(8,128)(2,1)S(1)} %collective-permute-done.7.refs_1_), channel_id=1, source_target_pairs={{0,4},{2,6},{4,0},{6,2},{8,12},{10,14},{12,8},{14,10},{16,20},{18,... | collective-permute-start | bytes 786440 | tf_op jit(solution)/shard_map/ppermute | solution.py:295
  81.1 0.5 collective-permute-start.11
  81.6 0.9 collective-permute-done.8.refs_2_
  82.5 4.2 %collective-permute-done.9.refs_3_ = bf16[4,32,1024]{2,1,0:T(8,128)(2,1)S(1)} collective-permute-done((bf16[4,32,1024]{2,1,0:T(8,128)(2,1)S(1)}, bf16[4,32,1024]{2,1,0:T(8,128)(2,1)S(1)}, u32[]{:S(2)}, u32[]{:S(2)}) %collective-permute-start.9) | collective-permute-done | bytes 262176 | tf_op jit(solution)/shard_map/ppermute | solution.py:295
  86.7 1.5 %collective-permute-done.13.refs_7_ = bf16[4,32,1024]{2,1,0:T(8,128)(2,1)S(1)} collective-permute-done((bf16[4,32,1024]{2,1,0:T(8,128)(2,1)S(1)}, bf16[4,32,1024]{2,1,0:T(8,128)(2,1)S(1)}, u32[]{:S(2)}, u32[]{:S(2)}) %collective-permute-start.13) | collective-permute-done | bytes 262176 | tf_op jit(solution)/shard_map/ppermute | solution.py:432
  88.2 1.4 %assemble.1.rotation = bf16[1024,1024]{1,0:T(8,128)(2,1)S(1)} custom-call(s32[3]{0:T(128)S(1)} %pad_add_fusion.place, bf16[4,32,1024]{2,1,0:T(8,128)(2,1)S(1)} %join.1.refs_0_, bf16[4,32,1024]{2,1,0:T(8,128)(2,1)S(1)} %collective-permute-done.7.refs_1_, bf16[4,32,1024]{2,1,0:T(8,128)(2,1)S(1)} %collective-permute-done.8.refs_2_, ...), custom_call_target="tpu_custom_call" | custom-call | flops 536870912 | bytes 4194304 | tf_op jit(solution)/shard_map/assemble/pallas_call | solution.py:323
  89.6 1.6 %rotate.1 = bf16[256,1024]{1,0:T(8,128)(2,1)} custom-call(bf16[16,2,64,128]{3,2,1,0:T(8,128)(2,1)S(1)} %all-to-all-done.1.filtered, bf16[1024,1024]{1,0:T(8,128)(2,1)S(1)} %assemble.1.rotation), custom_call_target="tpu_custom_call" | custom-call | tf_op jit(solution)/shard_map/rotate/pallas_call | solution.py:364
  (15 shorter events, 0.1 us)
Async XLA Ops:
  2.9 23.4 %all-to-all-start = ((bf16[16,2,64,128]{3,2,1,0:T(8,128)(2,1)}), bf16[16,2,64,128]{3,2,1,0:T(8,128)(2,1)S(1)}, u32[]{:S(2)}, u32[]{:S(2)}) async-start(bf16[16,2,64,128]{3,2,1,0:T(8,128)(2,1)} %get-tuple-element.17), calls=%async_computation | async-start | bytes 1048576 | tf_op jit(solution)/shard_map/all_to_all | solution.py:394
  26.4 5.3 %copy-start = (s32[32,8]{0,1:T(8,128)S(1)}, s32[32,8]{0,1:T(8,128)}, u32[]{:S(2)}) copy-start(s32[32,8]{0,1:T(8,128)} %param.7) | copy-start | bytes 3076
  26.4 5.3 %collective-permute-start = (bf16[2,64,128]{2,1,0:T(8,128)(2,1)S(1)}, bf16[2,64,128]{2,1,0:T(8,128)(2,1)S(1)}, u32[]{:S(2)}, u32[]{:S(2)}) collective-permute-start(bf16[2,64,128]{2,1,0:T(8,128)(2,1)S(1)} %constant_dynamic-slice_fusion), channel_id=1, source_target_pairs={{0,1},{1,0},{2,3},{3,2},{4,5},{5,4},{6,7},{7,6},{8,9},{9,8},{10,11... | collective-permute-start | bytes 98312 | tf_op jit(solution)/shard_map/ppermute | solution.py:285
  36.1 1.4 %collective-permute-start.1 = (bf16[2,64,128]{2,1,0:T(8,128)(2,1)S(1)}, bf16[2,64,128]{2,1,0:T(8,128)(2,1)S(1)}, u32[]{:S(2)}, u32[]{:S(2)}) collective-permute-start(bf16[2,64,128]{2,1,0:T(8,128)(2,1)S(1)} %get-tuple-element.19.refs_4_), channel_id=1, source_target_pairs={{0,1},{1,0},{2,3},{3,2},{4,5},{5,4},{6,7},{7,6},{8,9},{9,8},{10,11... | collective-permute-start | bytes 98312 | tf_op jit(solution)/shard_map/ppermute | solution.py:285
  40.4 1.3 %collective-permute-start.2 = (bf16[2,64,128]{2,1,0:T(8,128)(2,1)S(1)}, bf16[2,64,128]{2,1,0:T(8,128)(2,1)S(1)}, u32[]{:S(2)}, u32[]{:S(2)}) collective-permute-start(bf16[2,64,128]{2,1,0:T(8,128)(2,1)S(1)} %get-tuple-element.23), channel_id=1, source_target_pairs={{0,1},{1,0},{2,3},{3,2},{4,5},{5,4},{6,7},{7,6},{8,9},{9,8},{10,11... | collective-permute-start | bytes 98312 | tf_op jit(solution)/shard_map/ppermute | solution.py:285
  44.5 1.3 %collective-permute-start.3 = (bf16[2,64,128]{2,1,0:T(8,128)(2,1)S(1)}, bf16[2,64,128]{2,1,0:T(8,128)(2,1)S(1)}, u32[]{:S(2)}, u32[]{:S(2)}) collective-permute-start(bf16[2,64,128]{2,1,0:T(8,128)(2,1)S(1)} %get-tuple-element.26), channel_id=1, source_target_pairs={{0,1},{1,0},{2,3},{3,2},{4,5},{5,4},{6,7},{7,6},{8,9},{9,8},{10,11... | collective-permute-start | bytes 98312 | tf_op jit(solution)/shard_map/ppermute | solution.py:285
  49.3 40.3 %all-to-all-start.1 = ((bf16[16,2,64,128]{3,2,1,0:T(8,128)(2,1)}), bf16[16,2,64,128]{3,2,1,0:T(8,128)(2,1)S(1)}, u32[]{:S(2)}, u32[]{:S(2)}) async-start(bf16[16,2,64,128]{3,2,1,0:T(8,128)(2,1)} %bitcast.15), calls=%async_computation.1 | async-start | bytes 1048576 | tf_op jit(solution)/shard_map/all_to_all | solution.py:429
  53.3 11.6 %collective-permute-start.4 = (bf16[1,32,1024]{2,1,0:T(8,128)(2,1)S(1)}, bf16[1,32,1024]{2,1,0:T(8,128)(2,1)S(1)}, u32[]{:S(2)}, u32[]{:S(2)}) collective-permute-start(bf16[1,32,1024]{2,1,0:T(8,128)(2,1)S(1)} %get-tuple-element.28.refs_0_), channel_id=1, source_target_pairs={{0,8},{2,10},{4,12},{6,14},{8,0},{10,2},{12,4},{14,6},{16,24},{18,... | collective-permute-start | bytes 196616 | tf_op jit(solution)/shard_map/ppermute | solution.py:295
  55.2 17.9 %collective-permute-start.5 = (bf16[1,32,1024]{2,1,0:T(8,128)(2,1)S(1)}, bf16[1,32,1024]{2,1,0:T(8,128)(2,1)S(1)}, u32[]{:S(2)}, u32[]{:S(2)}) collective-permute-start(bf16[1,32,1024]{2,1,0:T(8,128)(2,1)S(1)} %get-tuple-element.28.refs_0_), channel_id=1, source_target_pairs={{0,16},{2,18},{4,20},{6,22},{8,24},{10,26},{12,28},{14,30},{16,0},... | collective-permute-start | bytes 196616 | tf_op jit(solution)/shard_map/ppermute | solution.py:295
  57.6 15.5 %collective-permute-start.6 = (bf16[1,32,1024]{2,1,0:T(8,128)(2,1)S(1)}, bf16[1,32,1024]{2,1,0:T(8,128)(2,1)S(1)}, u32[]{:S(2)}, u32[]{:S(2)}) collective-permute-start(bf16[1,32,1024]{2,1,0:T(8,128)(2,1)S(1)} %get-tuple-element.28.refs_0_), channel_id=1, source_target_pairs={{0,24},{2,26},{4,28},{6,30},{8,16},{10,18},{12,20},{14,22},{16,8},... | collective-permute-start | bytes 196616 | tf_op jit(solution)/shard_map/ppermute | solution.py:295
  73.1 6.5 %collective-permute-start.7 = (bf16[4,32,1024]{2,1,0:T(8,128)(2,1)S(1)}, bf16[4,32,1024]{2,1,0:T(8,128)(2,1)S(1)}, u32[]{:S(2)}, u32[]{:S(2)}) collective-permute-start(bf16[4,32,1024]{2,1,0:T(8,128)(2,1)S(1)} %join.1.refs_0_), channel_id=1, source_target_pairs={{0,2},{2,0},{4,6},{6,4},{8,10},{10,8},{12,14},{14,12},{16,18},{18,... | collective-permute-start | bytes 786440 | tf_op jit(solution)/shard_map/ppermute | solution.py:295
  74.6 7.8 %collective-permute-start.8 = (bf16[4,32,1024]{2,1,0:T(8,128)(2,1)S(1)}, bf16[4,32,1024]{2,1,0:T(8,128)(2,1)S(1)}, u32[]{:S(2)}, u32[]{:S(2)}) collective-permute-start(bf16[4,32,1024]{2,1,0:T(8,128)(2,1)S(1)} %join.1.refs_0_), channel_id=1, source_target_pairs={{0,4},{2,6},{4,0},{6,2},{8,12},{10,14},{12,8},{14,10},{16,20},{18,... | collective-permute-start | bytes 786440 | tf_op jit(solution)/shard_map/ppermute | solution.py:295
  79.6 7.0 %collective-permute-start.9 = (bf16[4,32,1024]{2,1,0:T(8,128)(2,1)S(1)}, bf16[4,32,1024]{2,1,0:T(8,128)(2,1)S(1)}, u32[]{:S(2)}, u32[]{:S(2)}) collective-permute-start(bf16[4,32,1024]{2,1,0:T(8,128)(2,1)S(1)} %collective-permute-done.7.refs_1_), channel_id=1, source_target_pairs={{0,4},{2,6},{4,0},{6,2},{8,12},{10,14},{12,8},{14,10},{16,20},{18,... | collective-permute-start | bytes 786440 | tf_op jit(solution)/shard_map/ppermute | solution.py:295
  81.1 5.6 %collective-permute-start.10 = (bf16[4,32,1024]{2,1,0:T(8,128)(2,1)S(1)}, bf16[4,32,1024]{2,1,0:T(8,128)(2,1)S(1)}, u32[]{:S(2)}, u32[]{:S(2)}) collective-permute-start(bf16[4,32,1024]{2,1,0:T(8,128)(2,1)S(1)} %join.1.refs_0_), channel_id=1, source_target_pairs={{0,1},{1,0},{2,3},{3,2},{4,5},{5,4},{6,7},{7,6},{8,9},{9,8},{10,11... | collective-permute-start | bytes 786440 | tf_op jit(solution)/shard_map/ppermute | solution.py:432
  81.1 5.6 %collective-permute-start.11 = (bf16[4,32,1024]{2,1,0:T(8,128)(2,1)S(1)}, bf16[4,32,1024]{2,1,0:T(8,128)(2,1)S(1)}, u32[]{:S(2)}, u32[]{:S(2)}) collective-permute-start(bf16[4,32,1024]{2,1,0:T(8,128)(2,1)S(1)} %collective-permute-done.7.refs_1_), channel_id=1, source_target_pairs={{0,1},{1,0},{2,3},{3,2},{4,5},{5,4},{6,7},{7,6},{8,9},{9,8},{10,11... | collective-permute-start | bytes 786440 | tf_op jit(solution)/shard_map/ppermute | solution.py:432
  82.5 4.2 %collective-permute-start.12 = (bf16[4,32,1024]{2,1,0:T(8,128)(2,1)S(1)}, bf16[4,32,1024]{2,1,0:T(8,128)(2,1)S(1)}, u32[]{:S(2)}, u32[]{:S(2)}) collective-permute-start(bf16[4,32,1024]{2,1,0:T(8,128)(2,1)S(1)} %collective-permute-done.8.refs_2_), channel_id=1, source_target_pairs={{0,1},{1,0},{2,3},{3,2},{4,5},{5,4},{6,7},{7,6},{8,9},{9,8},{10,11... | collective-permute-start | bytes 786440 | tf_op jit(solution)/shard_map/ppermute | solution.py:432
  86.6 1.5 %collective-permute-start.13 = (bf16[4,32,1024]{2,1,0:T(8,128)(2,1)S(1)}, bf16[4,32,1024]{2,1,0:T(8,128)(2,1)S(1)}, u32[]{:S(2)}, u32[]{:S(2)}) collective-permute-start(bf16[4,32,1024]{2,1,0:T(8,128)(2,1)S(1)} %collective-permute-done.9.refs_3_), channel_id=1, source_target_pairs={{0,1},{1,0},{2,3},{3,2},{4,5},{5,4},{6,7},{7,6},{8,9},{9,8},{10,11... | collective-permute-start | bytes 786440 | tf_op jit(solution)/shard_map/ppermute | solution.py:432
